TPU v7x, 128 devices: a whole 4x4x4 slice. The times are simulated.
128 devices in a mesh: row: 8 (over z, core), col: 16 (over x, y).
Axes of the slice: x: 4, y: 4, z: 4, core: 2. Of those that a mesh axis runs over, the one named last changes fastest.
Arguments:
- block_values: bfloat16 [8, 16, 256, 128, 128], P('row', 'col'), may hold values from -1.2 to 1.2
- block_rows: int32 [8, 16, 256], P('row', 'col'), may hold values from 0 to 207, as said below
- block_cols: int32 [8, 16, 256], P('row', 'col'), may hold values from 0 to 103, as said below
- start_vectors: bfloat16 [212992, 256], P(('row', 'col')), may hold values from -6 to 6
- center: float32 [1], replicated, may hold values from -0.5 to -0.1
- half_width: float32 [1], replicated, may hold values from 0.9 to 1.3
- row_counts: int32 [128], replicated, may hold values from 7 to 19, as said below
Outputs:
- relaid: bfloat16 [311296, 256], P(('row', 'col'))
Inputs may be any that keep to these rules, and one draw needn't show every extreme that they name: `block_rows`: the first 13 entries of cell (r, c) are its diagonal blocks, at local row c * 13 + k; the rest are anywhere; positions may repeat, and repeated blocks add. `block_cols`: the first 13 entries of cell (r, c) are at local column r * 13 + k. `row_counts`: entries 2 i and 2 i + 1 sum to 26; entry 0 is larger than 13.
All inputs are finite; a program needn't handle non-finite values.
Results may differ from a plain program's by a relative error of at most 0.019.
Values may be sent and summed in bfloat16 or wider, within the bound.
A program may use at most 192 MiB of HBM per device.

v0:
```python
import math

import jax
import jax.numpy as jnp
from jax import lax
from jax.sharding import PartitionSpec as P


def swapped(block, axis, bit):
    count = lax.axis_size(axis)
    route = []
    for low in range(count):
        high = low | 1 << bit
        if high != low and high < count:
            route += [(low, high), (high, low)]
    return lax.ppermute(block, axis, route)


def block_images(values, row_ids, col_ids, panel_rows, out_blocks):
    orbitals = values.shape[-1]
    vec_count = panel_rows.shape[-1]
    blocks = panel_rows.reshape(-1, orbitals, vec_count)
    block_count = values.shape[0]
    group_size = math.gcd(block_count, 64)

    def add_group(row_images, group_items):
        group_values, group_rows, group_cols = group_items
        picked = blocks[group_cols]
        images = jnp.einsum(
            "gij,gjv->giv", group_values, picked, preferred_element_type=jnp.float32
        )
        return (row_images.at[group_rows].add(images), None)

    initial = jnp.zeros((out_blocks, orbitals, vec_count), jnp.float32)
    turns = block_count // group_size
    group_items = (
        values.reshape(turns, group_size, orbitals, orbitals),
        row_ids.reshape(turns, group_size),
        col_ids.reshape(turns, group_size),
    )
    row_images, _ = lax.scan(add_group, initial, group_items)
    return row_images.reshape(out_blocks * orbitals, vec_count)


def on_device(block_values, block_rows, block_cols, start_vectors, center, half_width, row_counts):
    orbitals = block_values.shape[-1]
    values = block_values.reshape(-1, orbitals, orbitals)
    row_ids = block_rows.reshape(-1)
    col_ids = block_cols.reshape(-1)
    own_rows, vec_count = start_vectors.shape
    own_blocks = own_rows // orbitals
    col_count = lax.axis_size("col")
    center_value = center[0]
    width_value = half_width[0]

    def image_of(vectors):
        panel_rows = lax.all_gather(vectors, "row", axis=0, tiled=True)
        cell_terms = block_images(values, row_ids, col_ids, panel_rows, col_count * own_blocks)
        return lax.psum_scatter(
            cell_terms.astype(jnp.bfloat16), "col", scatter_dimension=0, tiled=True
        ).astype(jnp.float32)

    source = start_vectors.astype(jnp.float32)
    first_image = image_of(start_vectors)
    first_step = ((first_image - center_value * source) / width_value).astype(jnp.bfloat16)
    second_image = image_of(first_step)
    second = (
        2.0 * (second_image - center_value * first_step.astype(jnp.float32)) / width_value - source
    ).astype(jnp.bfloat16)
    device = lax.axis_index("row") * col_count + lax.axis_index("col")
    parity = device % 2
    even_count = row_counts[device - parity]
    own_count = row_counts[device]
    start_block = parity * even_count
    half_blocks = own_blocks // 2
    capacity = own_blocks + half_blocks
    partner = swapped(second, ("row", "col"), 0)
    window = jnp.where(
        parity == 0, jnp.concatenate([second, partner], 0), jnp.concatenate([partner, second], 0)
    )
    window_low = parity * 0
    padded = jnp.concatenate([window, jnp.zeros((capacity * orbitals, vec_count), jnp.bfloat16)], 0)
    selected = lax.dynamic_slice_in_dim(padded, start_block * orbitals, capacity * orbitals, 0)
    live_rows = jnp.arange(capacity * orbitals, dtype=jnp.int32)[:, None] < own_count * orbitals
    return jnp.where(live_rows, selected, jnp.zeros_like(selected))


def solution(mesh):
    placed = (
        P("row", "col", None, None, None),
        P("row", "col", None),
        P("row", "col", None),
        P(("row", "col"), None),
        P(),
        P(),
        P(),
    )
    return jax.shard_map(
        on_device, mesh=mesh, in_specs=placed, out_specs=P(("row", "col"), None), check_vma=False
    )
```

profile of v0, /device:TPU:8, one launch (start us, length us, event | category | flops | bytes accessed | tf_op | source)
XLA Modules:
  0.0 644.4 jit_solution(17980662493797626057)
XLA Ops:
  10.6 44.0 %all-gather.3.cloned.1.call-done = bf16[13312,256]{1,0:T(8,128)(2,1)} async-done(((bf16[1664,256]{1,0:T(8,128)(2,1)}), bf16[13312,256]{1,0:T(8,128)(2,1)}) %all-gather.3.cloned.1.call-update) | async-done | bytes 6815760 | tf_op jit(solution)/shard_map/all_gather | solution.py:57
  54.6 12.5 %broadcast.88.clone = f32[208,128,256]{2,1,0:T(8,128)} broadcast(f32[]{:T(128)} %constant.61.clone.1), dimensions={} | broadcast | bytes 27262980 | tf_op jit(solution)/shard_map/broadcast.15
  67.1 131.1 %while.20 = (s32[]{:T(128)}, f32[208,128,256]{2,1,0:T(8,128)}, s32[4,64]{1,0:T(4,128)S(1)}, bf16[4,64,128,128]{3,2,1,0:T(8,128)(2,1)}, s32[4,64]{1,0:T(4,128)S(1)}, /*index=5*/bf16[104,128,256]{2,1,0:T(8,128)(2,1)}, s32[]{:T(128)}) while((s32[]{:T(128)}, f32[208,128,256]{2,1,0:T(8,128)}, s32[4,64]{1,0:T(4,128)S(1)}, ...), condition=%wide.region_2.3_spmd, body=%wide.region_0.2_spmd.sunk | while | flops 538969472 | bytes 48240976 | solution.py:41
  67.1 5.7 gather_fusion
  72.8 7.3 %fusion.35 = f32[64,128,256]{2,1,0:T(8,128)} fusion(bf16[64,128,256]{2,1,0:T(8,128)(2,1)} %gather_fusion, bf16[4,64,128,128]{3,2,1,0:T(8,128)(2,1)} %get-tuple-element.200, s32[]{:T(128)} %get-tuple-element.190), kind=kOutput, calls=%fused_computation.4.clone.1 | convolution fusion | flops 536870912 | bytes 14680576 | tf_op jit(solution)/shard_map/while/body/eval_jaxpr/gij,gjv->giv/dot_general | solution.py:29
  80.1 19.9 %scatter_fusion = f32[208,128,256]{2,1,0:T(8,128)} fusion(f32[208,128,256]{2,1,0:T(8,128)} %get-tuple-element.191, s32[64]{0:T(128)S(1)} %get-tuple-element.173, f32[64,128,256]{2,1,0:T(8,128)} %fusion.35), kind=kCustom, calls=%fused_computation.2.clone.1 | custom fusion | flops 2097152 | bytes 25166080 | tf_op jit(solution)/shard_map/while/body/eval_jaxpr/scatter-add | solution.py:32
  100.0 5.7 gather_fusion
  105.7 7.3 %fusion.35 = f32[64,128,256]{2,1,0:T(8,128)} fusion(bf16[64,128,256]{2,1,0:T(8,128)(2,1)} %gather_fusion, bf16[4,64,128,128]{3,2,1,0:T(8,128)(2,1)} %get-tuple-element.200, s32[]{:T(128)} %get-tuple-element.190), kind=kOutput, calls=%fused_computation.4.clone.1 | convolution fusion | flops 536870912 | bytes 14680576 | tf_op jit(solution)/shard_map/while/body/eval_jaxpr/gij,gjv->giv/dot_general | solution.py:29
  113.0 19.7 %scatter_fusion = f32[208,128,256]{2,1,0:T(8,128)} fusion(f32[208,128,256]{2,1,0:T(8,128)} %get-tuple-element.191, s32[64]{0:T(128)S(1)} %get-tuple-element.173, f32[64,128,256]{2,1,0:T(8,128)} %fusion.35), kind=kCustom, calls=%fused_computation.2.clone.1 | custom fusion | flops 2097152 | bytes 25166080 | tf_op jit(solution)/shard_map/while/body/eval_jaxpr/scatter-add | solution.py:32
  132.8 5.7 gather_fusion
  138.5 7.3 %fusion.35 = f32[64,128,256]{2,1,0:T(8,128)} fusion(bf16[64,128,256]{2,1,0:T(8,128)(2,1)} %gather_fusion, bf16[4,64,128,128]{3,2,1,0:T(8,128)(2,1)} %get-tuple-element.200, s32[]{:T(128)} %get-tuple-element.190), kind=kOutput, calls=%fused_computation.4.clone.1 | convolution fusion | flops 536870912 | bytes 14680576 | tf_op jit(solution)/shard_map/while/body/eval_jaxpr/gij,gjv->giv/dot_general | solution.py:29
  145.8 19.8 %scatter_fusion = f32[208,128,256]{2,1,0:T(8,128)} fusion(f32[208,128,256]{2,1,0:T(8,128)} %get-tuple-element.191, s32[64]{0:T(128)S(1)} %get-tuple-element.173, f32[64,128,256]{2,1,0:T(8,128)} %fusion.35), kind=kCustom, calls=%fused_computation.2.clone.1 | custom fusion | flops 2097152 | bytes 25166080 | tf_op jit(solution)/shard_map/while/body/eval_jaxpr/scatter-add | solution.py:32
  165.6 5.7 gather_fusion
  171.3 7.3 %fusion.35 = f32[64,128,256]{2,1,0:T(8,128)} fusion(bf16[64,128,256]{2,1,0:T(8,128)(2,1)} %gather_fusion, bf16[4,64,128,128]{3,2,1,0:T(8,128)(2,1)} %get-tuple-element.200, s32[]{:T(128)} %get-tuple-element.190), kind=kOutput, calls=%fused_computation.4.clone.1 | convolution fusion | flops 536870912 | bytes 14680576 | tf_op jit(solution)/shard_map/while/body/eval_jaxpr/gij,gjv->giv/dot_general | solution.py:29
  178.6 19.6 %scatter_fusion = f32[208,128,256]{2,1,0:T(8,128)} fusion(f32[208,128,256]{2,1,0:T(8,128)} %get-tuple-element.191, s32[64]{0:T(128)S(1)} %get-tuple-element.173, f32[64,128,256]{2,1,0:T(8,128)} %fusion.35), kind=kCustom, calls=%fused_computation.2.clone.1 | custom fusion | flops 2097152 | bytes 25166080 | tf_op jit(solution)/shard_map/while/body/eval_jaxpr/scatter-add | solution.py:32
  198.2 15.5 %convert_element_type.30 = bf16[208,128,256]{2,1,0:T(8,128)(2,1)} convert(f32[208,128,256]{2,1,0:T(8,128)} %get-tuple-element.69) | non-fusion elementwise | flops 6815744 | bytes 40894464 | tf_op jit(solution)/shard_map/convert_element_type | solution.py:60
  215.2 95.7 %reduce-scatter.3.cloned.1.call-done = bf16[1664,256]{1,0:T(8,128)(2,1)} async-done(((bf16[26624,256]{1,0:T(8,128)(2,1)}), bf16[1664,256]{1,0:T(8,128)(2,1)}) %reduce-scatter.3.cloned.1.call-update) | async-done | bytes 851984 | tf_op jit(solution)/shard_map/reduce_scatter | solution.py:59
  313.3 43.1 %all-gather.5.cloned.1.call-done = bf16[13312,256]{1,0:T(8,128)(2,1)} async-done(((bf16[1664,256]{1,0:T(8,128)(2,1)}), bf16[13312,256]{1,0:T(8,128)(2,1)}) %all-gather.5.cloned.1.call-update) | async-done | bytes 6815760 | tf_op jit(solution)/shard_map/all_gather | solution.py:57
  356.3 12.5 %broadcast.88 = f32[208,128,256]{2,1,0:T(8,128)} broadcast(f32[]{:T(128)} %constant.61.clone.1), dimensions={} | broadcast | bytes 27262980 | tf_op jit(solution)/shard_map/broadcast.15
  368.8 131.1 %while.21 = (s32[]{:T(128)}, f32[208,128,256]{2,1,0:T(8,128)}, s32[4,64]{1,0:T(4,128)S(1)}, bf16[4,64,128,128]{3,2,1,0:T(8,128)(2,1)}, s32[4,64]{1,0:T(4,128)S(1)}, /*index=5*/bf16[104,128,256]{2,1,0:T(8,128)(2,1)}, s32[]{:T(128)}) while((s32[]{:T(128)}, f32[208,128,256]{2,1,0:T(8,128)}, s32[4,64]{1,0:T(4,128)S(1)}, ...), condition=%wide.region_6.7_spmd, body=%wide.region_4.6_spmd.sunk | while | flops 538969472 | bytes 48240976 | solution.py:41
  374.5 7.3 %fusion.39 = f32[64,128,256]{2,1,0:T(8,128)} fusion(bf16[64,128,256]{2,1,0:T(8,128)(2,1)} %gather_fusion.1, bf16[4,64,128,128]{3,2,1,0:T(8,128)(2,1)} %get-tuple-element.221, s32[]{:T(128)} %get-tuple-element.211), kind=kOutput, calls=%fused_computation.17.clone.1 | convolution fusion | flops 536870912 | bytes 14680576 | tf_op jit(solution)/shard_map/while/body/eval_jaxpr/gij,gjv->giv/dot_general | solution.py:29
  381.8 19.9 %scatter_fusion.1 = f32[208,128,256]{2,1,0:T(8,128)} fusion(f32[208,128,256]{2,1,0:T(8,128)} %get-tuple-element.212, s32[64]{0:T(128)S(1)} %get-tuple-element.181, f32[64,128,256]{2,1,0:T(8,128)} %fusion.39), kind=kCustom, calls=%fused_computation.3.clone.1 | custom fusion | flops 2097152 | bytes 25166080 | tf_op jit(solution)/shard_map/while/body/eval_jaxpr/scatter-add | solution.py:32
  407.4 7.3 %fusion.39 = f32[64,128,256]{2,1,0:T(8,128)} fusion(bf16[64,128,256]{2,1,0:T(8,128)(2,1)} %gather_fusion.1, bf16[4,64,128,128]{3,2,1,0:T(8,128)(2,1)} %get-tuple-element.221, s32[]{:T(128)} %get-tuple-element.211), kind=kOutput, calls=%fused_computation.17.clone.1 | convolution fusion | flops 536870912 | bytes 14680576 | tf_op jit(solution)/shard_map/while/body/eval_jaxpr/gij,gjv->giv/dot_general | solution.py:29
  414.7 19.7 %scatter_fusion.1 = f32[208,128,256]{2,1,0:T(8,128)} fusion(f32[208,128,256]{2,1,0:T(8,128)} %get-tuple-element.212, s32[64]{0:T(128)S(1)} %get-tuple-element.181, f32[64,128,256]{2,1,0:T(8,128)} %fusion.39), kind=kCustom, calls=%fused_computation.3.clone.1 | custom fusion | flops 2097152 | bytes 25166080 | tf_op jit(solution)/shard_map/while/body/eval_jaxpr/scatter-add | solution.py:32
  434.5 5.7 gather_fusion.1
  440.2 7.3 %fusion.39 = f32[64,128,256]{2,1,0:T(8,128)} fusion(bf16[64,128,256]{2,1,0:T(8,128)(2,1)} %gather_fusion.1, bf16[4,64,128,128]{3,2,1,0:T(8,128)(2,1)} %get-tuple-element.221, s32[]{:T(128)} %get-tuple-element.211), kind=kOutput, calls=%fused_computation.17.clone.1 | convolution fusion | flops 536870912 | bytes 14680576 | tf_op jit(solution)/shard_map/while/body/eval_jaxpr/gij,gjv->giv/dot_general | solution.py:29
  447.5 19.8 %scatter_fusion.1 = f32[208,128,256]{2,1,0:T(8,128)} fusion(f32[208,128,256]{2,1,0:T(8,128)} %get-tuple-element.212, s32[64]{0:T(128)S(1)} %get-tuple-element.181, f32[64,128,256]{2,1,0:T(8,128)} %fusion.39), kind=kCustom, calls=%fused_computation.3.clone.1 | custom fusion | flops 2097152 | bytes 25166080 | tf_op jit(solution)/shard_map/while/body/eval_jaxpr/scatter-add | solution.py:32
  473.0 7.3 %fusion.39 = f32[64,128,256]{2,1,0:T(8,128)} fusion(bf16[64,128,256]{2,1,0:T(8,128)(2,1)} %gather_fusion.1, bf16[4,64,128,128]{3,2,1,0:T(8,128)(2,1)} %get-tuple-element.221, s32[]{:T(128)} %get-tuple-element.211), kind=kOutput, calls=%fused_computation.17.clone.1 | convolution fusion | flops 536870912 | bytes 14680576 | tf_op jit(solution)/shard_map/while/body/eval_jaxpr/gij,gjv->giv/dot_general | solution.py:29
  480.3 19.6 %scatter_fusion.1 = f32[208,128,256]{2,1,0:T(8,128)} fusion(f32[208,128,256]{2,1,0:T(8,128)} %get-tuple-element.212, s32[64]{0:T(128)S(1)} %get-tuple-element.181, f32[64,128,256]{2,1,0:T(8,128)} %fusion.39), kind=kCustom, calls=%fused_computation.3.clone.1 | custom fusion | flops 2097152 | bytes 25166080 | tf_op jit(solution)/shard_map/while/body/eval_jaxpr/scatter-add | solution.py:32
  499.9 15.5 %convert_element_type.35 = bf16[208,128,256]{2,1,0:T(8,128)(2,1)} convert(f32[208,128,256]{2,1,0:T(8,128)} %get-tuple-element.70) | non-fusion elementwise | flops 6815744 | bytes 40894464 | tf_op jit(solution)/shard_map/convert_element_type | solution.py:60
  515.4 96.9 %reduce-scatter.5.cloned.1.call-done = bf16[1664,256]{1,0:T(8,128)(2,1)} async-done(((bf16[26624,256]{1,0:T(8,128)(2,1)}), bf16[1664,256]{1,0:T(8,128)(2,1)}) %reduce-scatter.5.cloned.1.call-update) | async-done | bytes 851984 | tf_op jit(solution)/shard_map/reduce_scatter | solution.py:59
  617.7 16.7 %collective-permute-done = bf16[1664,256]{1,0:T(8,128)(2,1)S(1)} collective-permute-done((bf16[1664,256]{1,0:T(8,128)(2,1)S(1)}, bf16[1664,256]{1,0:T(8,128)(2,1)S(1)}, u32[]{:S(2)}, u32[]{:S(2)}) %collective-permute-start) | collective-permute-done | bytes 852000 | tf_op jit(solution)/shard_map/ppermute | solution.py:16
  (45 shorter events, 31.4 us)
Async XLA Ops:
  6.5 48.1 %all-gather.3.cloned.1.call-start = ((), (), s32[]{:S(2)}) async-start(), calls=%async_computation.2 | async-start | bytes 7667712 | tf_op jit(solution)/shard_map/all_gather | solution.py:57
  7.3 303.6 %reduce-scatter.3.cloned.1.call-start = ((), (), s32[]{:S(2)}) async-start(), calls=%async_computation.3 | async-start | bytes 14483456 | tf_op jit(solution)/shard_map/reduce_scatter | solution.py:59
  213.7 97.1 %copy-start = (bf16[1664,256]{1,0:T(8,128)(2,1)S(1)}, bf16[1664,256]{1,0:T(8,128)(2,1)}, u32[]{:S(2)}) copy-start(bf16[1664,256]{1,0:T(8,128)(2,1)} %param.14) | copy-start | bytes 2555908
  213.7 142.6 %all-gather.5.cloned.1.call-start = ((), (), s32[]{:S(2)}) async-start(), calls=%async_computation.4 | async-start | bytes 7667712 | tf_op jit(solution)/shard_map/all_gather | solution.py:57
  313.2 299.2 %reduce-scatter.5.cloned.1.call-start = ((), (), s32[]{:S(2)}) async-start(), calls=%async_computation.5 | async-start | bytes 14483456 | tf_op jit(solution)/shard_map/reduce_scatter | solution.py:59
  515.4 97.0 %copy-start.1 = (bf16[1664,256]{1,0:T(8,128)(2,1)S(1)}, bf16[1664,256]{1,0:T(8,128)(2,1)}, u32[]{:S(2)}) copy-start(bf16[1664,256]{1,0:T(8,128)(2,1)} %reduce-scatter.3.cloned.1.call-done) | copy-start | bytes 2555908
  515.4 100.4 %copy-start.2 = (s32[128]{0:T(128)S(1)}, s32[128]{0:T(128)}, u32[]{:S(2)}) copy-start(s32[128]{0:T(128)} %param.17) | copy-start | bytes 1540
  614.3 20.1 %collective-permute-start = (bf16[1664,256]{1,0:T(8,128)(2,1)S(1)}, bf16[1664,256]{1,0:T(8,128)(2,1)S(1)}, u32[]{:S(2)}, u32[]{:S(2)}) collective-permute-start(bf16[1664,256]{1,0:T(8,128)(2,1)S(1)} %fusion.19), channel_id=1, source_target_pairs={{0,1},{1,0},{2,3},{3,2},{4,5},{5,4},{6,7},{7,6},{8,9},{9,8},{10,11... | collective-permute-start | bytes 2555912 | tf_op jit(solution)/shard_map/ppermute | solution.py:16
Sparse Core Ops, SparseCore 0:
  9.0 45.5 all-gather.2
  213.9 96.8 reduce-scatter.2
  313.3 42.9 all-gather.4
  515.6 96.7 reduce-scatter.4
where the time goes:
time: 647 us; the launch traced here: 644 us
  waiting for transfers between devices  297 us (46%)
  other arithmetic  200 us (31%)
  local copies, waits for them, and re-layouts  71.9 us (11%)
  matrix products  58.4 us (9%)
  between operations  15.8 us (2%)
    reduce_scatter x2, waiting for transfers between devices, image_of(): lax.psum_scatter(cell_terms.astype(jnp.bfloat16), 'col', scatter_dimensio...  193 us
    scatter-add x8, other arithmetic, add_group(): return (row_images.at[group_rows].add(images), None)  158 us
    all_gather x2, waiting for transfers between devices, image_of(): panel_rows = lax.all_gather(vectors, 'row', axis=0, tiled=True)  87 us
    dot_general x8, matrix products, add_group(): jnp.einsum('gij,gjv->giv', group_values, picked, preferred_element_type=j...  58.4 us
    gather x8, local copies, waits for them, and re-layouts, add_group(): picked = blocks[group_cols]  45.7 us
    convert_element_type x2, other arithmetic, image_of(): cell_terms.astype(jnp.bfloat16)  31.1 us
    another operation x2, local copies, waits for them, and re-layouts  24.9 us
    ppermute x1, waiting for transfers between devices, swapped(): return lax.ppermute(block, axis, route)  16.7 us
  transfers between devices with their start and end apart: 5, of which 5 were waited for; matrix products, arithmetic and copies ran while one was open for 1% of the time, Pallas kernels for 0%

commit v1 on v0

v1 whole, which is shorter than its diff:
```python
import functools

import jax
import jax.numpy as jnp
from jax import lax
from jax.experimental import pallas as pl
from jax.experimental.pallas import tpu as pltpu
from jax.sharding import PartitionSpec as P

ORB = 128
VECS = 256
BD = 13
MOVE = 6
GROUP = 16


def product_kernel(rows_ref, cols_ref, values_ref, panel_hbm, out_hbm, acc, panel, stage, panel_sem, out_sem):
    step = pl.program_id(0)
    steps = pl.num_programs(0)
    dests = acc.shape[0] // BD

    @pl.when(step == 0)
    def _():
        copy = pltpu.make_async_copy(panel_hbm, panel, panel_sem)
        copy.start()

        @pl.loop(0, acc.shape[0])
        def _(i):
            acc[i] = jnp.zeros((ORB, VECS), jnp.float32)

        copy.wait()

    for e in range(GROUP):
        row = rows_ref[step * GROUP + e]
        col = cols_ref[step * GROUP + e]
        acc[row] += jnp.dot(values_ref[e], panel[col], preferred_element_type=jnp.float32)

    @pl.when(step == steps - 1)
    def _():
        def out_copy(d, slot):
            return pltpu.make_async_copy(stage.at[slot], out_hbm.at[pl.ds(d * BD, BD)], out_sem.at[slot])

        for d in range(dests):
            slot = d % 2
            if d >= 2:
                out_copy(d - 2, slot).wait()

            @pl.loop(0, BD)
            def _(b):
                stage[slot, b] = acc[d * BD + b].astype(jnp.bfloat16)

            out_copy(d, slot).start()
        for d in range(dests - 2, dests):
            out_copy(d, d % 2).wait()


def cell_terms(values, row_ids, col_ids, panel_rows, out_blocks):
    count = values.shape[0]
    panel = panel_rows.reshape(-1, ORB, VECS)
    out = pl.pallas_call(
        product_kernel,
        out_shape=jax.ShapeDtypeStruct((out_blocks, ORB, VECS), jnp.bfloat16),
        grid_spec=pltpu.PrefetchScalarGridSpec(
            num_scalar_prefetch=2,
            grid=(count // GROUP,),
            in_specs=[
                pl.BlockSpec((GROUP, ORB, ORB), lambda s, r, c: (s, 0, 0)),
                pl.BlockSpec(memory_space=pl.ANY),
            ],
            out_specs=pl.BlockSpec(memory_space=pl.ANY),
            scratch_shapes=[
                pltpu.VMEM((out_blocks, ORB, VECS), jnp.float32),
                pltpu.VMEM(panel.shape, jnp.bfloat16),
                pltpu.VMEM((2, BD, ORB, VECS), jnp.bfloat16),
                pltpu.SemaphoreType.DMA,
                pltpu.SemaphoreType.DMA((2,)),
            ],
        ),
        compiler_params=pltpu.CompilerParams(
            dimension_semantics=("arbitrary",), vmem_limit_bytes=56 * 1024 * 1024
        ),
        name="block_products",
    )(row_ids, col_ids, values, panel)
    return out.reshape(out_blocks * ORB, VECS)


def swapped(block, axis):
    count = lax.axis_size(axis)
    return lax.ppermute(block, axis, [(i, i ^ 1) for i in range(count)])


def on_device(block_values, block_rows, block_cols, start_vectors, center, half_width, row_counts):
    values = block_values.reshape(-1, ORB, ORB)
    row_ids = block_rows.reshape(-1)
    col_ids = block_cols.reshape(-1)
    col_count = lax.axis_size("col")
    center_value = center[0]
    width_value = half_width[0]

    def image_of(vectors):
        panel_rows = lax.all_gather(vectors, "row", axis=0, tiled=True)
        terms = cell_terms(values, row_ids, col_ids, panel_rows, col_count * BD)
        return lax.psum_scatter(terms, "col", scatter_dimension=0, tiled=True).astype(jnp.float32)

    source = start_vectors.astype(jnp.float32)
    first_image = image_of(start_vectors)
    first_step = ((first_image - center_value * source) / width_value).astype(jnp.bfloat16)
    second_image = image_of(first_step)
    second = (
        2.0 * (second_image - center_value * first_step.astype(jnp.float32)) / width_value - source
    ).astype(jnp.bfloat16)
    device = lax.axis_index("row") * col_count + lax.axis_index("col")
    parity = device % 2
    even_count = row_counts[device - parity]
    own_count = row_counts[device]
    start_block = jnp.where(parity == 0, 0, even_count - (BD - MOVE))
    capacity = BD + MOVE
    leaving = lax.dynamic_slice_in_dim(second, (1 - parity) * ((BD - MOVE) * ORB), MOVE * ORB, 0)
    arriving = swapped(leaving, ("row", "col"))
    window = jnp.where(
        parity == 0, jnp.concatenate([second, arriving], 0), jnp.concatenate([arriving, second], 0)
    )
    padded = jnp.concatenate([window, jnp.zeros((2 * MOVE * ORB, VECS), jnp.bfloat16)], 0)
    selected = lax.dynamic_slice_in_dim(padded, start_block * ORB, capacity * ORB, 0)
    live_rows = jnp.arange(capacity * ORB, dtype=jnp.int32)[:, None] < own_count * ORB
    return jnp.where(live_rows, selected, jnp.zeros_like(selected))


def solution(mesh):
    placed = (
        P("row", "col", None, None, None),
        P("row", "col", None),
        P("row", "col", None),
        P(("row", "col"), None),
        P(),
        P(),
        P(),
    )
    return jax.shard_map(
        on_device, mesh=mesh, in_specs=placed, out_specs=P(("row", "col"), None), check_vma=False
    )
```

time: 647 us -> 369 us (0.57)
  other arithmetic: 200 us -> 7.88 us
  local copies, waits for them, and re-layouts: 71.9 us -> 0.7 us
  matrix products: 58.4 us -> 0 us
  Pallas kernels: 0 us -> 50 us
    scatter-add x8 -> x0, other arithmetic: 158 us -> none  [add_group(): return (row_images.at[group_rows].add(images), None)]
    dot_general x8 -> x0, matrix products: 58.4 us -> none  [add_group(): jnp.einsum('gij,gjv->giv', group_values, picked, preferred_element_type=j...]
    pallas_call x0 -> x2, Pallas kernels: none -> 50 us  [cell_terms(): pl.pallas_call(product_kernel, out_shape=jax.ShapeDtypeStruct((out_blocks...]
    gather x8 -> x0, local copies, waits for them, and re-layouts: 45.7 us -> none  [add_group(): picked = blocks[group_cols]]
    convert_element_type x2 -> x0, other arithmetic: 31.1 us -> none  [image_of(): cell_terms.astype(jnp.bfloat16)]
    another operation x4 -> x0, local copies, waits for them, and re-layouts: 25.1 us -> none
    ppermute x1, waiting for transfers between devices: 16.7 us -> 6.79 us  [swapped(): return lax.ppermute(block, axis, [(i, i ^ 1) for i in range(count)])]
  transfers between devices with their start and end apart: 5 -> 5, of which waited for: 5 -> 5; matrix products, arithmetic and copies ran while one was open for 1% -> 0% of each run, Pallas kernels for 0% -> 0%
where the time goes in v1:
time: 369 us; the launch traced here: 367 us
  waiting for transfers between devices  291 us (79%)
  Pallas kernels  50 us (14%)
  between operations  15.8 us (4%)
  other arithmetic  7.88 us (2%)
    reduce_scatter x2, waiting for transfers between devices, image_of(): lax.psum_scatter(terms, 'col', scatter_dimension=0, tiled=True)  193 us
    all_gather x2, waiting for transfers between devices, image_of(): panel_rows = lax.all_gather(vectors, 'row', axis=0, tiled=True)  90.2 us
    pallas_call x2, Pallas kernels, cell_terms(): pl.pallas_call(product_kernel, out_shape=jax.ShapeDtypeStruct((out_blocks...  50 us
  transfers between devices with their start and end apart: 5, of which 5 were waited for; matrix products, arithmetic and copies ran while one was open for 0% of the time, Pallas kernels for 0%

profile of v1, /device:TPU:8, one launch (start us, length us, event | category | flops | bytes accessed | tf_op | source)
XLA Modules:
  0.0 366.9 jit_solution(4335498512121896696)
XLA Ops:
  6.5 0.0 all-gather.3.cloned.1.call-start
  6.5 0.7 all-gather.3.cloned.1.call-update
  7.3 0.0 reduce-scatter.3.cloned.1.call-start
  7.3 47.3 %all-gather.3.cloned.1.call-done = bf16[13312,256]{1,0:T(8,128)(2,1)} async-done(((bf16[1664,256]{1,0:T(8,128)(2,1)}), bf16[13312,256]{1,0:T(8,128)(2,1)}) %all-gather.3.cloned.1.call-update) | async-done | bytes 6815760 | tf_op jit(solution)/shard_map/all_gather | solution.py:101
  54.6 25.0 %block_products.2 = bf16[208,128,256]{2,1,0:T(8,128)(2,1)} custom-call(s32[256]{0:T(256)} %bitcast.21, s32[256]{0:T(256)} %bitcast.23, bf16[256,128,128]{2,1,0:T(8,128)(2,1)} %bitcast.17, bf16[104,128,256]{2,1,0:T(8,128)(2,1)} %bitcast.20), custom_call_target="tpu_custom_call" | custom-call | tf_op jit(solution)/shard_map/block_products/pallas_call | solution.py:60
  79.6 0.0 copy-start
  79.6 0.0 reduce-scatter.3.cloned.1.call-update
  79.6 0.0 all-gather.5.cloned.1.call-start
  81.0 95.9 %reduce-scatter.3.cloned.1.call-done = bf16[1664,256]{1,0:T(8,128)(2,1)} async-done(((bf16[26624,256]{1,0:T(8,128)(2,1)}), bf16[1664,256]{1,0:T(8,128)(2,1)}) %reduce-scatter.3.cloned.1.call-update) | async-done | bytes 851984 | tf_op jit(solution)/shard_map/reduce_scatter | solution.py:103
  176.9 0.0 copy-done
  176.9 2.4 fusion.2
  179.3 0.0 all-gather.5.cloned.1.call-update
  179.3 0.0 reduce-scatter.5.cloned.1.call-start
  179.4 42.9 %all-gather.5.cloned.1.call-done = bf16[13312,256]{1,0:T(8,128)(2,1)} async-done(((bf16[1664,256]{1,0:T(8,128)(2,1)}), bf16[13312,256]{1,0:T(8,128)(2,1)}) %all-gather.5.cloned.1.call-update) | async-done | bytes 6815760 | tf_op jit(solution)/shard_map/all_gather | solution.py:101
  222.3 25.0 %block_products.3 = bf16[208,128,256]{2,1,0:T(8,128)(2,1)} custom-call(s32[256]{0:T(256)} %bitcast.22, s32[256]{0:T(256)} %bitcast.24, bf16[256,128,128]{2,1,0:T(8,128)(2,1)} %bitcast.18, bf16[104,128,256]{2,1,0:T(8,128)(2,1)} %bitcast.19), custom_call_target="tpu_custom_call" | custom-call | tf_op jit(solution)/shard_map/block_products/pallas_call | solution.py:60
  247.3 0.0 copy-start.1
  247.3 0.0 reduce-scatter.5.cloned.1.call-update
  247.3 97.4 %reduce-scatter.5.cloned.1.call-done = bf16[1664,256]{1,0:T(8,128)(2,1)} async-done(((bf16[26624,256]{1,0:T(8,128)(2,1)}), bf16[1664,256]{1,0:T(8,128)(2,1)}) %reduce-scatter.5.cloned.1.call-update) | async-done | bytes 851984 | tf_op jit(solution)/shard_map/reduce_scatter | solution.py:103
  344.7 0.0 copy-done.1
  344.7 0.0 copy-start.2
  344.7 1.9 fusion.3
  346.7 1.3 collective-permute-start
  348.0 0.0 copy-done.2
  348.0 0.7 fusion.5
  349.9 6.8 %collective-permute-done = bf16[768,256]{1,0:T(8,128)(2,1)S(1)} collective-permute-done((bf16[768,256]{1,0:T(8,128)(2,1)S(1)}, bf16[768,256]{1,0:T(8,128)(2,1)S(1)}, u32[]{:S(2)}, u32[]{:S(2)}) %collective-permute-start) | collective-permute-done | bytes 393248 | tf_op jit(solution)/shard_map/ppermute | solution.py:89
  356.7 0.5 maximum_select_fusion
  357.2 3.1 fusion.4
  (2 shorter events, 0.0 us)
Async XLA Ops:
  6.5 48.1 %all-gather.3.cloned.1.call-start = ((), (), s32[]{:S(2)}) async-start(), calls=%async_computation.2 | async-start | bytes 7667712 | tf_op jit(solution)/shard_map/all_gather | solution.py:101
  7.3 169.7 %reduce-scatter.3.cloned.1.call-start = ((), (), s32[]{:S(2)}) async-start(), calls=%async_computation.3 | async-start | bytes 14483456 | tf_op jit(solution)/shard_map/reduce_scatter | solution.py:103
  79.6 97.3 %copy-start = (bf16[1664,256]{1,0:T(8,128)(2,1)S(1)}, bf16[1664,256]{1,0:T(8,128)(2,1)}, u32[]{:S(2)}) copy-start(bf16[1664,256]{1,0:T(8,128)(2,1)} %param.10) | copy-start | bytes 2555908
  79.6 142.6 %all-gather.5.cloned.1.call-start = ((), (), s32[]{:S(2)}) async-start(), calls=%async_computation.4 | async-start | bytes 7667712 | tf_op jit(solution)/shard_map/all_gather | solution.py:101
  179.3 165.4 %reduce-scatter.5.cloned.1.call-start = ((), (), s32[]{:S(2)}) async-start(), calls=%async_computation.5 | async-start | bytes 14483456 | tf_op jit(solution)/shard_map/reduce_scatter | solution.py:103
  247.3 97.4 %copy-start.1 = (bf16[1664,256]{1,0:T(8,128)(2,1)S(1)}, bf16[1664,256]{1,0:T(8,128)(2,1)}, u32[]{:S(2)}) copy-start(bf16[1664,256]{1,0:T(8,128)(2,1)} %reduce-scatter.3.cloned.1.call-done) | copy-start | bytes 2555908
  344.7 3.3 copy-start.2
  346.7 10.1 %collective-permute-start = (bf16[768,256]{1,0:T(8,128)(2,1)S(1)}, bf16[768,256]{1,0:T(8,128)(2,1)S(1)}, u32[]{:S(2)}, u32[]{:S(2)}) collective-permute-start(bf16[768,256]{1,0:T(8,128)(2,1)S(1)} %constant_dynamic-slice_fusion), channel_id=1, source_target_pairs={{0,1},{1,0},{2,3},{3,2},{4,5},{5,4},{6,7},{7,6},{8,9},{9,8},{10,11... | collective-permute-start | bytes 1179656 | tf_op jit(solution)/shard_map/ppermute | solution.py:89
Sparse Core Ops, SparseCore 0:
  9.0 45.5 all-gather.2
  79.8 97.1 reduce-scatter.2
  179.4 42.7 all-gather.4
  247.4 97.2 reduce-scatter.4

commit v2 on v1

--- a/solution.py
+++ b/solution.py
@@ -84,9 +84,502 @@
     return out.reshape(out_blocks * ORB, VECS)
 
 
-def swapped(block, axis):
-    count = lax.axis_size(axis)
-    return lax.ppermute(block, axis, [(i, i ^ 1) for i in range(count)])
+MESH = pl.DeviceIdType.MESH
+SIDE = 4
+HALF = BD * ORB // 2
+GROUPS = 4
+PART = HALF // GROUPS
+PART_A = (PART // 32) * 16 + (PART % 32)
+PART_B = PART - PART_A
+RELAY_A, RELAY_B, DIRECT_A, DIRECT_B, SUM_A, SUM_B = range(6)
+STRIPE = 16
+
+
+def shifted(position, by):
+    return (position + by + SIDE) % SIDE
+
+
+class Place:
+    def __init__(self):
+        self.row = lax.axis_index("row")
+        self.col = lax.axis_index("col")
+        self.z, self.core = self.row // 2, self.row % 2
+        self.x, self.y = self.col // SIDE, self.col % SIDE
+
+    def along(self, axis, by):
+        if axis == 0:
+            return (self.row, shifted(self.x, by) * SIDE + self.y)
+        if axis == 1:
+            return (self.row, self.x * SIDE + shifted(self.y, by))
+        return (self.slot(by), self.col)
+
+    def slot(self, by):
+        return shifted(self.z, by) * 2 + self.core
+
+    def partner(self):
+        return (self.z * 2 + 1 - self.core, self.col)
+
+    def greet(self, targets):
+        barrier = pltpu.get_barrier_semaphore()
+        for target in targets:
+            pl.semaphore_signal(barrier, inc=1, device_id=target, device_id_type=MESH)
+        pl.semaphore_wait(barrier, len(targets))
+
+
+def remote(src, dst, send_sem, recv_sem, target):
+    return pltpu.make_async_remote_copy(
+        src_ref=src, dst_ref=dst, send_sem=send_sem, recv_sem=recv_sem, device_id=target, device_id_type=MESH
+    )
+
+
+def part_rows(group, kind):
+    return pl.ds(pl.multiple_of(kind * HALF + group * PART, 16), PART)
+
+
+def stripes(rows, body):
+    @pl.loop(0, rows // STRIPE)
+    def _(i):
+        body(pl.multiple_of(i * STRIPE, STRIPE))
+
+
+def wide(value):
+    return value.astype(jnp.float32)
+
+
+class Gather:
+    def __init__(self, place, own, panel, send_sem, recv_sem):
+        self.place, self.own, self.panel = place, own, panel
+        self.send_sem, self.recv_sem = send_sem, recv_sem
+
+    def copy(self, group, kind, index):
+        place = self.place
+        rows = part_rows(group, kind)
+        plus, minus, partner = place.along(2, 1), place.along(2, -1), place.partner()
+        mine, below, above, far = place.slot(0), place.slot(-1), place.slot(1), place.slot(2)
+        own = self.own.at[rows]
+        slot, target = [
+            (mine, plus),
+            (mine, minus),
+            (mine, partner),
+            (below, plus) if kind == 0 else (above, minus),
+            (below, partner),
+            (above, partner),
+            (far, partner),
+        ][index]
+        source = own if index < 3 else self.panel.at[slot, rows]
+        sems = (group, kind, index)
+        return remote(source, self.panel.at[slot, rows], self.send_sem.at[sems], self.recv_sem.at[sems], target)
+
+    def first(self, group):
+        for index in range(3):
+            for kind in range(2):
+                self.copy(group, kind, index).start()
+
+    def second(self, group):
+        for kind in range(2):
+            self.copy(group, kind, 0).wait_recv()
+            self.copy(group, kind, 1).wait_recv()
+            for index in (3, 4, 5):
+                self.copy(group, kind, index).start()
+
+    def third(self, group):
+        for kind in range(2):
+            self.copy(group, kind, 3).wait_recv()
+            self.copy(group, kind, 6).start()
+
+    def fourth(self, group):
+        for kind in range(2):
+            for index in (2, 4, 5, 6):
+                self.copy(group, kind, index).wait_recv()
+
+    def close(self, group):
+        for kind in range(2):
+            for index in range(7):
+                self.copy(group, kind, index).wait_send()
+
+
+def panel_out(panel, out_hbm, out_sem, group, kind):
+    rows = part_rows(group, kind)
+    return pltpu.make_async_copy(panel.at[:, rows], out_hbm.at[:, rows], out_sem.at[group, kind])
+
+
+def gather_kernel(start_hbm, out_hbm, panel, load_sem, out_sem, send_sem, recv_sem):
+    place = Place()
+    own = panel.at[place.slot(0)]
+    gather = Gather(place, own, panel, send_sem, recv_sem)
+    load = pltpu.make_async_copy(start_hbm, own, load_sem)
+    load.start()
+    place.greet([place.along(2, 1), place.along(2, -1), place.partner()])
+    load.wait()
+    for it in range(GROUPS + 3):
+        if it < GROUPS:
+            gather.first(it)
+        if 0 <= it - 1 < GROUPS:
+            gather.second(it - 1)
+        if 0 <= it - 2 < GROUPS:
+            gather.third(it - 2)
+        if 0 <= it - 3 < GROUPS:
+            gather.fourth(it - 3)
+            for kind in range(2):
+                panel_out(panel, out_hbm, out_sem, it - 3, kind).start()
+    for group in range(GROUPS):
+        gather.close(group)
+        for kind in range(2):
+            panel_out(panel, out_hbm, out_sem, group, kind).wait()
+
+
+class Reduce:
+    def __init__(self, place, terms, minus_sum, plus_sum, result, far_slots, near_a, near_b, load_sem, far_sems, near_sems):
+        self.place, self.terms = place, terms
+        self.sums = (minus_sum, plus_sum)
+        self.result, self.far_slots, self.near = result, far_slots, (near_a, near_b)
+        self.load_sem, self.far_sems, self.near_sems = load_sem, far_sems, near_sems
+
+    def position(self, axis):
+        return self.place.x if axis == 0 else self.place.y
+
+    def piece(self, group, kind, target, half):
+        rows = part_rows(group, kind)
+        span = pl.ds(0, SIDE) if half is None else pl.ds(2 * half, 2)
+        if kind == 0:
+            return self.terms.at[target, span, rows]
+        return self.terms.at[span, target, rows]
+
+    def load(self, group, kind, index):
+        p = self.position(kind)
+        sem = self.load_sem.at[group, kind, index]
+        if index == 0:
+            return pltpu.make_async_copy(self.piece(group, kind, shifted(p, -1), 0), self.sums[0].at[group, kind], sem)
+        if index == 1:
+            return pltpu.make_async_copy(self.piece(group, kind, shifted(p, 1), 1), self.sums[1].at[group, kind], sem)
+        return pltpu.make_async_copy(self.piece(group, kind, p, None), self.result.at[group, kind], sem)
+
+    def far(self, group, kind, index):
+        p = self.position(kind)
+        if index == RELAY_A:
+            source, by = self.piece(group, kind, shifted(p, 2), 0), -1
+        elif index == RELAY_B:
+            source, by = self.piece(group, kind, shifted(p, 2), 1), 1
+        elif index == DIRECT_B:
+            source, by = self.piece(group, kind, shifted(p, -1), 1), -1
+        elif index == DIRECT_A:
+            source, by = self.piece(group, kind, shifted(p, 1), 0), 1
+        elif index == SUM_A:
+            source, by = self.sums[0].at[group, kind], -1
+        else:
+            source, by = self.sums[1].at[group, kind], 1
+        sems = (group, kind, index)
+        return remote(
+            source,
+            self.far_slots.at[sems],
+            self.far_sems[0].at[sems],
+            self.far_sems[1].at[sems],
+            self.place.along(kind, by),
+        )
+
+    def near_piece(self, group, kind, target, half):
+        rows = pl.ds(0, PART_A) if half == 0 else pl.ds(PART_A, PART_B)
+        return self.result.at[group, kind, target, rows]
+
+    def near_copy(self, group, kind, index):
+        axis = 1 - kind
+        p = self.position(axis)
+        half, by, to = {
+            RELAY_A: (0, -1, 2),
+            RELAY_B: (1, 1, 2),
+            DIRECT_B: (1, -1, -1),
+            DIRECT_A: (0, 1, 1),
+            SUM_A: (0, -1, -1),
+            SUM_B: (1, 1, 1),
+        }[index]
+        source = self.near_piece(group, kind, shifted(p, to), half)
+        sems = (group, kind, index)
+        return remote(
+            source,
+            self.near[half].at[group, kind, index // 2],
+            self.near_sems[0].at[sems],
+            self.near_sems[1].at[sems],
+            self.place.along(axis, by),
+        )
+
+    def neighbours(self):
+        return [self.place.along(axis, by) for axis in (0, 1) for by in (1, -1)]
+
+    def loads(self, group):
+        for kind in range(2):
+            for index in range(3):
+                self.load(group, kind, index).start()
+
+    def far_start(self, group):
+        for index in (RELAY_A, RELAY_B, DIRECT_A, DIRECT_B):
+            for kind in range(2):
+                self.far(group, kind, index).start()
+
+    def far_relay(self, group):
+        for kind in range(2):
+            for side, (arrived, leaving) in enumerate(((RELAY_A, SUM_A), (RELAY_B, SUM_B))):
+                self.load(group, kind, side).wait()
+                self.far(group, kind, arrived).wait_recv()
+                total = self.sums[side]
+
+                def body(at, total=total, kind=kind, arrived=arrived):
+                    rows = pl.ds(at, STRIPE)
+                    value = wide(total[group, kind, :, rows]) + wide(self.far_slots[group, kind, arrived, :, rows])
+                    total[group, kind, :, rows] = value.astype(jnp.bfloat16)
+
+                stripes(PART, body)
+                self.far(group, kind, leaving).start()
+
+    def far_total(self, group):
+        for kind in range(2):
+            self.load(group, kind, 2).wait()
+            for index in (DIRECT_A, DIRECT_B, SUM_A, SUM_B):
+                self.far(group, kind, index).wait_recv()
+
+            def body(at, kind=kind):
+                rows = pl.ds(at, STRIPE)
+                for half, (one, two) in enumerate(((DIRECT_A, SUM_A), (DIRECT_B, SUM_B))):
+                    own = pl.ds(2 * half, 2)
+                    value = (
+                        wide(self.result[group, kind, own, rows])
+                        + wide(self.far_slots[group, kind, one, :, rows])
+                        + wide(self.far_slots[group, kind, two, :, rows])
+                    )
+                    self.result[group, kind, own, rows] = value.astype(jnp.bfloat16)
+
+            stripes(PART, body)
+            for index in (RELAY_A, RELAY_B, DIRECT_A, DIRECT_B):
+                self.near_copy(group, kind, index).start()
+
+    def near_relay(self, group):
+        for kind in range(2):
+            p = self.position(1 - kind)
+            for half, (arrived, leaving, to) in enumerate(((RELAY_A, SUM_A, -1), (RELAY_B, SUM_B, 1))):
+                self.near_copy(group, kind, arrived).wait_recv()
+                first = half * PART_A
+                target = shifted(p, to)
+                slots = self.near[half]
+
+                def body(at, kind=kind, first=first, target=target, slots=slots):
+                    rows = pl.ds(first + at, STRIPE)
+                    value = wide(self.result[group, kind, target, rows]) + wide(slots[group, kind, 0, pl.ds(at, STRIPE)])
+                    self.result[group, kind, target, rows] = value.astype(jnp.bfloat16)
+
+                stripes((PART_A, PART_B)[half], body)
+                self.near_copy(group, kind, leaving).start()
+
+    def near_total(self, group, finish):
+        for kind in range(2):
+            p = self.position(1 - kind)
+            for half, (one, two) in enumerate(((DIRECT_A, SUM_A), (DIRECT_B, SUM_B))):
+                self.near_copy(group, kind, one).wait_recv()
+                self.near_copy(group, kind, two).wait_recv()
+                first = half * PART_A
+                slots = self.near[half]
+                base = kind * HALF + group * PART + first
+
+                def body(at, kind=kind, first=first, slots=slots, base=base):
+                    here = pl.ds(at, STRIPE)
+                    value = (
+                        wide(self.result[group, kind, p, pl.ds(first + at, STRIPE)])
+                        + wide(slots[group, kind, 1, here])
+                        + wide(slots[group, kind, 2, here])
+                    )
+                    finish(pl.ds(pl.multiple_of(base + at, STRIPE), STRIPE), value)
+
+                stripes((PART_A, PART_B)[half], body)
+
+    def close(self, group):
+        for kind in range(2):
+            for index in range(6):
+                self.far(group, kind, index).wait_send()
+                self.near_copy(group, kind, index).wait_send()
+
+
+def first_kernel(center, width, terms, start_hbm, out_hbm, panel, source, source_sem, out_sem, gather_send, gather_recv, *scratch):
+    place = Place()
+    own = panel.at[place.slot(0)]
+    gather = Gather(place, own, panel, gather_send, gather_recv)
+    reduce = reducer(place, terms, scratch)
+    load = pltpu.make_async_copy(start_hbm, source, source_sem)
+    for group in range(GROUPS):
+        reduce.loads(group)
+    load.start()
+    place.greet(reduce.neighbours() + [place.along(2, 1), place.along(2, -1), place.partner()])
+    mine = place.slot(0)
+
+    def finish(rows, image):
+        value = (image - center[0] * wide(source[rows])) / width[0]
+        panel[mine, rows] = value.astype(jnp.bfloat16)
+
+    def opened(group):
+        if group == 0:
+            load.wait()
+        reduce.near_total(group, finish)
+        gather.first(group)
+
+    def landed(group):
+        gather.fourth(group)
+        for kind in range(2):
+            panel_out(panel, out_hbm, out_sem, group, kind).start()
+
+    stages = [reduce.far_start, reduce.far_relay, reduce.far_total, reduce.near_relay, opened, gather.second, gather.third, landed]
+    run(stages)
+    for group in range(GROUPS):
+        reduce.close(group)
+        gather.close(group)
+        for kind in range(2):
+            panel_out(panel, out_hbm, out_sem, group, kind).wait()
+
+
+def second_kernel(center, width, terms, start_hbm, panel_hbm, out_hbm, arriving, source, first, value_out, load_sem, out_sem, swap_sem, *scratch):
+    place = Place()
+    reduce = reducer(place, terms, scratch)
+    loads = [
+        pltpu.make_async_copy(start_hbm, source, load_sem.at[0]),
+        pltpu.make_async_copy(panel_hbm.at[place.slot(0)], first, load_sem.at[1]),
+    ]
+    for group in range(GROUPS):
+        reduce.loads(group)
+    for load in loads:
+        load.start()
+    place.greet(reduce.neighbours())
+    parity = place.y % 2
+    other = (place.row, place.x * SIDE + place.y + 1 - 2 * parity)
+
+    def finish(rows, image):
+        value = 2.0 * (image - center[0] * wide(first[rows])) / width[0] - wide(source[rows])
+        value_out[rows] = value.astype(jnp.bfloat16)
+
+    def swap(group):
+        rows = pl.ds(pl.multiple_of((1 - parity) * HALF + group * PART, 16), PART)
+        here = pl.ds(group * PART, PART)
+        return remote(value_out.at[rows], arriving.at[here], swap_sem.at[0, group], swap_sem.at[1, group], other)
+
+    def out_copy(group, kind):
+        rows = part_rows(group, kind)
+        return pltpu.make_async_copy(value_out.at[rows], out_hbm.at[rows], out_sem.at[group, kind])
+
+    def opened(group):
+        if group == 0:
+            for load in loads:
+                load.wait()
+        reduce.near_total(group, finish)
+        swap(group).start()
+        for kind in range(2):
+            out_copy(group, kind).start()
+
+    run([reduce.far_start, reduce.far_relay, reduce.far_total, reduce.near_relay, opened])
+    for group in range(GROUPS):
+        reduce.close(group)
+        swap(group).wait()
+        for kind in range(2):
+            out_copy(group, kind).wait()
+
+
+def run(stages):
+    for it in range(GROUPS + len(stages) - 1):
+        for lag, stage in enumerate(stages):
+            if 0 <= it - lag < GROUPS:
+                stage(it - lag)
+
+
+def reducer(place, terms, scratch):
+    minus_sum, plus_sum, result, far_slots, near_a, near_b, load_sem, far_s, far_r, near_s, near_r = scratch
+    return Reduce(
+        place, terms, minus_sum, plus_sum, result, far_slots, near_a, near_b, load_sem, (far_s, far_r), (near_s, near_r)
+    )
+
+
+def reduce_scratch():
+    bf16 = jnp.bfloat16
+    dma = pltpu.SemaphoreType.DMA
+    return [
+        pltpu.VMEM((GROUPS, 2, 2, PART, VECS), bf16),
+        pltpu.VMEM((GROUPS, 2, 2, PART, VECS), bf16),
+        pltpu.VMEM((GROUPS, 2, SIDE, PART, VECS), bf16),
+        pltpu.VMEM((GROUPS, 2, 6, 2, PART, VECS), bf16),
+        pltpu.VMEM((GROUPS, 2, 3, PART_A, VECS), bf16),
+        pltpu.VMEM((GROUPS, 2, 3, PART_B, VECS), bf16),
+        dma((GROUPS, 2, 3)),
+        dma((GROUPS, 2, 6)),
+        dma((GROUPS, 2, 6)),
+        dma((GROUPS, 2, 6)),
+        dma((GROUPS, 2, 6)),
+    ]
+
+
+ROWS = BD * ORB
+ANY = pl.BlockSpec(memory_space=pl.ANY)
+SCALAR = pl.BlockSpec(memory_space=pltpu.SMEM)
+
+
+def comm_call(kernel, name, collective_id, in_specs, out_shape, scratch):
+    return pl.pallas_call(
+        kernel,
+        out_shape=out_shape,
+        in_specs=in_specs,
+        out_specs=jax.tree.map(lambda _: ANY, out_shape),
+        scratch_shapes=scratch,
+        compiler_params=pltpu.CompilerParams(
+            collective_id=collective_id, has_side_effects=True, vmem_limit_bytes=48 * 1024 * 1024
+        ),
+        name=name,
+    )
+
+
+def panel_shape(row_count):
+    return jax.ShapeDtypeStruct((row_count, ROWS, VECS), jnp.bfloat16)
+
+
+def gather_scratch():
+    dma = pltpu.SemaphoreType.DMA
+    return [dma((GROUPS, 2)), dma((GROUPS, 2, 7)), dma((GROUPS, 2, 7))]
+
+
+def gathered(start, row_count):
+    return comm_call(
+        gather_kernel,
+        "gather_rows",
+        0,
+        [ANY],
+        panel_shape(row_count),
+        [pltpu.VMEM((row_count, ROWS, VECS), jnp.bfloat16), pltpu.SemaphoreType.DMA] + gather_scratch(),
+    )(start)
+
+
+def first_of(center, width, terms, start, row_count):
+    return comm_call(
+        first_kernel,
+        "reduce_and_gather",
+        1,
+        [SCALAR, SCALAR, ANY, ANY],
+        panel_shape(row_count),
+        [
+            pltpu.VMEM((row_count, ROWS, VECS), jnp.bfloat16),
+            pltpu.VMEM((ROWS, VECS), jnp.bfloat16),
+            pltpu.SemaphoreType.DMA,
+        ]
+        + gather_scratch()
+        + reduce_scratch(),
+    )(center, width, terms.reshape(SIDE, SIDE, ROWS, VECS), start)
+
+
+def second_of(center, width, terms, start, panel):
+    dma = pltpu.SemaphoreType.DMA
+    return comm_call(
+        second_kernel,
+        "reduce_and_swap",
+        2,
+        [SCALAR, SCALAR, ANY, ANY, ANY],
+        (
+            jax.ShapeDtypeStruct((ROWS, VECS), jnp.bfloat16),
+            jax.ShapeDtypeStruct((HALF, VECS), jnp.bfloat16),
+        ),
+        [pltpu.VMEM((ROWS, VECS), jnp.bfloat16)] * 3
+        + [dma((2,)), dma((GROUPS, 2)), dma((2, GROUPS))]
+        + reduce_scratch(),
+    )(center, width, terms.reshape(SIDE, SIDE, ROWS, VECS), start, panel)
 
 
 def on_device(block_values, block_rows, block_cols, start_vectors, center, half_width, row_counts):
@@ -94,35 +587,27 @@
     row_ids = block_rows.reshape(-1)
     col_ids = block_cols.reshape(-1)
     col_count = lax.axis_size("col")
-    center_value = center[0]
-    width_value = half_width[0]
-
-    def image_of(vectors):
-        panel_rows = lax.all_gather(vectors, "row", axis=0, tiled=True)
-        terms = cell_terms(values, row_ids, col_ids, panel_rows, col_count * BD)
-        return lax.psum_scatter(terms, "col", scatter_dimension=0, tiled=True).astype(jnp.float32)
-
-    source = start_vectors.astype(jnp.float32)
-    first_image = image_of(start_vectors)
-    first_step = ((first_image - center_value * source) / width_value).astype(jnp.bfloat16)
-    second_image = image_of(first_step)
-    second = (
-        2.0 * (second_image - center_value * first_step.astype(jnp.float32)) / width_value - source
-    ).astype(jnp.bfloat16)
+    row_count = lax.axis_size("row")
+    out_blocks = col_count * BD
+
+    panel = gathered(start_vectors, row_count)
+    terms = cell_terms(values, row_ids, col_ids, panel, out_blocks)
+    panel = first_of(center, half_width, terms, start_vectors, row_count)
+    terms = cell_terms(values, row_ids, col_ids, panel, out_blocks)
+    second, arriving = second_of(center, half_width, terms, start_vectors, panel)
+
     device = lax.axis_index("row") * col_count + lax.axis_index("col")
     parity = device % 2
     even_count = row_counts[device - parity]
     own_count = row_counts[device]
-    start_block = jnp.where(parity == 0, 0, even_count - (BD - MOVE))
-    capacity = BD + MOVE
-    leaving = lax.dynamic_slice_in_dim(second, (1 - parity) * ((BD - MOVE) * ORB), MOVE * ORB, 0)
-    arriving = swapped(leaving, ("row", "col"))
+    start_row = jnp.where(parity == 0, 0, even_count * ORB - HALF)
+    capacity = (BD + MOVE) * ORB
     window = jnp.where(
         parity == 0, jnp.concatenate([second, arriving], 0), jnp.concatenate([arriving, second], 0)
     )
-    padded = jnp.concatenate([window, jnp.zeros((2 * MOVE * ORB, VECS), jnp.bfloat16)], 0)
-    selected = lax.dynamic_slice_in_dim(padded, start_block * ORB, capacity * ORB, 0)
-    live_rows = jnp.arange(capacity * ORB, dtype=jnp.int32)[:, None] < own_count * ORB
+    padded = jnp.concatenate([window, jnp.zeros((capacity, VECS), jnp.bfloat16)], 0)
+    selected = lax.dynamic_slice_in_dim(padded, start_row, capacity, 0)
+    live_rows = jnp.arange(capacity, dtype=jnp.int32)[:, None] < own_count * ORB
     return jnp.where(live_rows, selected, jnp.zeros_like(selected))
 
 

time: 369 us -> 282 us (0.76)
  waiting for transfers between devices: 291 us -> 0 us
  Pallas kernels: 50 us -> 271 us
  between operations: 15.8 us -> 2.65 us
  other arithmetic: 7.88 us -> 3.42 us
    pallas_call x0 -> x3, Pallas kernels: none -> 221 us  [the longest x1 101 us: first_of(): comm_call(first_kernel, 'reduce_and_gather', 1, [SCALAR, SCALAR, ANY, ANY...]
    reduce_scatter x2 -> x0, waiting for transfers between devices: 193 us -> none  [image_of(): lax.psum_scatter(terms, 'col', scatter_dimension=0, tiled=True)]
    all_gather x2 -> x0, waiting for transfers between devices: 90.2 us -> none  [image_of(): panel_rows = lax.all_gather(vectors, 'row', axis=0, tiled=True)]
    ppermute x1 -> x0, waiting for transfers between devices: 6.79 us -> none  [swapped(): return lax.ppermute(block, axis, [(i, i ^ 1) for i in range(count)])]
    convert_element_type x2 -> x0, other arithmetic: 4.28 us -> none  [the longest x1 2.37 us: on_device(): ((first_image - center_value * source) / width_value).astype(jnp.bfloat16)]
  transfers between devices with their start and end apart: 5 -> 0, of which waited for: 5 -> 0; matrix products, arithmetic and copies ran while one was open for 0% -> 0% of each run, Pallas kernels for 0% -> 0%
where the time goes in v2:
time: 282 us; the launch traced here: 280 us
  Pallas kernels  271 us (96%)
  other arithmetic  3.42 us (1%)
    pallas_call x1, Pallas kernels, first_of(): comm_call(first_kernel, 'reduce_and_gather', 1, [SCALAR, SCALAR, ANY, ANY...  101 us
    pallas_call x1, Pallas kernels, second_of(): comm_call(second_kernel, 'reduce_and_swap', 2, [SCALAR, SCALAR, ANY, ANY,...  84.3 us
    pallas_call x2, Pallas kernels, cell_terms(): pl.pallas_call(product_kernel, out_shape=jax.ShapeDtypeStruct((out_blocks...  50.1 us
    pallas_call x1, Pallas kernels, gathered(): comm_call(gather_kernel, 'gather_rows', 0, [ANY], panel_shape(row_count),...  36.1 us

profile of v2, /device:TPU:8, one launch (start us, length us, event | category | flops | bytes accessed | tf_op | source)
XLA Modules:
  0.0 279.9 jit_solution(11703861157579715399)
XLA Ops:
  0.0 1.3 fusion.1
  3.3 0.0 copy-start
  3.3 1.1 copy-done
  4.4 36.1 %gather_rows.1 = bf16[8,1664,256]{2,1,0:T(8,128)(2,1)} custom-call(bf16[1664,256]{1,0:T(8,128)(2,1)S(1)} %copy-done), custom_call_target="tpu_custom_call" | custom-call | tf_op jit(solution)/shard_map/gather_rows/pallas_call | solution.py:541
  40.6 0.0 copy-start.1
  40.6 25.1 %block_products.2 = bf16[208,128,256]{2,1,0:T(8,128)(2,1)} custom-call(s32[256]{0:T(256)} %bitcast.15, s32[256]{0:T(256)} %bitcast.17, bf16[256,128,128]{2,1,0:T(8,128)(2,1)} %bitcast.12, bf16[104,128,256]{2,1,0:T(8,128)(2,1)} %bitcast.14), custom_call_target="tpu_custom_call" | custom-call | tf_op jit(solution)/shard_map/block_products/pallas_call | solution.py:60
  65.7 0.0 copy-done.1
  65.7 100.8 %reduce_and_gather.1.panel_hbm = bf16[8,1664,256]{2,1,0:T(8,128)(2,1)} custom-call(f32[1]{0:T(128)S(6)} %copy.8.center, f32[1]{0:T(128)S(6)} %copy.9.width, bf16[4,4,1664,256]{3,2,1,0:T(8,128)(2,1)} %bitcast.11, bf16[1664,256]{1,0:T(8,128)(2,1)S(1)} %copy-done.1), custom_call_target="tpu_custom_call" | custom-call | tf_op jit(solution)/shard_map/reduce_and_gather/pallas_call | solution.py:552
  166.5 25.0 %block_products.3 = bf16[208,128,256]{2,1,0:T(8,128)(2,1)} custom-call(s32[256]{0:T(256)} %bitcast.16, s32[256]{0:T(256)} %bitcast.18, bf16[256,128,128]{2,1,0:T(8,128)(2,1)} %bitcast.13, bf16[104,128,256]{2,1,0:T(8,128)(2,1)} %bitcast.9), custom_call_target="tpu_custom_call" | custom-call | tf_op jit(solution)/shard_map/block_products/pallas_call | solution.py:60
  191.5 84.3 %reduce_and_swap.1 = (bf16[1664,256]{1,0:T(8,128)(2,1)S(1)}, bf16[832,256]{1,0:T(8,128)(2,1)S(1)}) custom-call(f32[1]{0:T(128)S(6)} %copy.8.center, f32[1]{0:T(128)S(6)} %copy.9.width, bf16[4,4,1664,256]{3,2,1,0:T(8,128)(2,1)} %bitcast.10, bf16[1664,256]{1,0:T(8,128)(2,1)S(1)} %copy-done.1, bf16[8,1664,256]{2,1,0:T(8,128)(2,1)} %reduce_and_gather.1.panel_hbm), custom_call_target="tpu_custom_call" | custom-call | tf_op jit(solution)/shard_map/reduce_and_swap/pallas_call | solution.py:570
  275.9 0.3 maximum_select_fusion
  276.8 3.1 %fusion = bf16[2432,256]{1,0:T(8,128)(2,1)} fusion(s32[]{:T(128)S(6)} %select_n.38, bf16[2496,256]{1,0:T(8,128)(2,1)S(1)} %maximum_select_fusion, pred[2432]{0:T(1024)(128)(4,1)S(1)} %iota_compare_fusion), kind=kLoop, calls=%fused_computation.2 | loop fusion | flops 622592 | bytes 2525572 | tf_op jit(solution)/shard_map/jit(_where)/select_n | solution.py:611
  (1 shorter events, 0.0 us)
Async XLA Ops:
  3.3 1.2 copy-start
  40.6 25.2 %copy-start.1 = (bf16[1664,256]{1,0:T(8,128)(2,1)S(1)}, bf16[1664,256]{1,0:T(8,128)(2,1)}, u32[]{:S(2)}) copy-start(bf16[1664,256]{1,0:T(8,128)(2,1)} %start_hbm.5) | copy-start | bytes 2555908

commit v3 on v0

v3 whole, which is shorter than its diff:
```python
import functools

import jax
import jax.numpy as jnp
from jax import lax
from jax.experimental import pallas as pl
from jax.experimental.pallas import tpu as pltpu
from jax.sharding import PartitionSpec as P

ORB = 128
VECS = 256
BD = 13
MOVE = 6
GROUP = 8


def product_kernel(codes_ref, values_ref, panel_ref, out_ref):
    @pl.loop(0, out_ref.shape[0])
    def _(i):
        out_ref[i] = jnp.zeros((ORB, VECS), jnp.bfloat16)

    def group(step, carry):
        before, total = carry
        for e in range(GROUP):
            code = codes_ref[step * GROUP + e]
            row, col, entry = code >> 15, (code >> 8) & 127, code & 255
            product = jnp.dot(values_ref[entry], panel_ref[col], preferred_element_type=jnp.float32)
            total = jnp.where(row == before, total, 0.0) + product
            out_ref[row] = total.astype(jnp.bfloat16)
            before = row
        return before, total

    lax.fori_loop(
        0, values_ref.shape[0] // GROUP, group, (jnp.int32(-1), jnp.zeros((ORB, VECS), jnp.float32))
    )


def entry_codes(row_ids, col_ids):
    count = row_ids.shape[0]
    codes = (row_ids * 128 + col_ids) * 256 + jnp.arange(count, dtype=jnp.int32)
    rank = jnp.sum((codes[None, :] < codes[:, None]).astype(jnp.int32), 1)
    here = rank[:, None] == jnp.arange(count, dtype=jnp.int32)[None, :]
    return jnp.sum(jnp.where(here, codes[:, None], 0), 0)


def cell_terms(codes, values, panel_rows, out_blocks):
    panel = panel_rows.reshape(-1, ORB, VECS)
    vmem = pl.BlockSpec(memory_space=pltpu.VMEM)
    return pl.pallas_call(
        product_kernel,
        out_shape=jax.ShapeDtypeStruct((out_blocks, ORB, VECS), jnp.bfloat16),
        in_specs=[pl.BlockSpec(memory_space=pltpu.SMEM), vmem, vmem],
        out_specs=vmem,
        compiler_params=pltpu.CompilerParams(vmem_limit_bytes=PRODUCT_LIMIT * 1024 * 1024),
        name="block_products",
    )(codes, values, panel)


PRODUCT_LIMIT = 10
MESH = pl.DeviceIdType.MESH
SIDE = 4
HALF = BD * ORB // 2
ROWS = BD * ORB
GATHER_PARTS = (416, 416)
FIRST_PARTS = (160, 176, 144, 112, 96, 80, 64)
SECOND_PARTS = (208, 352, 272)
RELAY_A, RELAY_B, DIRECT_A, DIRECT_B, SUM_A, SUM_B = range(6)
FIRST_ORDER = (
    0, 1, 32, 33, 2, 3, 64, 65, 34, 35, 66, 67, 96, 97, 4, 5, 98, 128, 129, 99,
    36, 37, 68, 161, 193, 130, 131, 160, 192, 69, 225, 6, 7, 224, 162, 194, 38, 39, 257, 100,
    256, 163, 195, 226, 101, 70, 71, 227, 8, 9, 133, 132, 258, 40, 41, 259, 102, 103, 72, 164,
    196, 165, 197, 73, 10, 135, 134, 228, 11, 42, 43, 12, 229, 13, 104, 166, 198, 260, 105, 261,
    167, 199, 74, 230, 75, 44, 45, 76, 231, 136, 137, 77, 262, 106, 263, 107, 168, 200, 108, 169,
    201, 138, 139, 109, 232, 140, 170, 202, 233, 171, 203, 141, 172, 204, 264, 234, 173, 205, 265, 235,
    236, 266, 237, 267, 268, 269,
)
SECOND_ORDER = (
    0, 1, 32, 33, 2, 3, 34, 35, 64, 65, 4, 5, 66, 67, 96, 97, 36, 37, 68, 69,
    98, 128, 129, 99, 100, 161, 130, 131, 160, 101, 163, 132, 133, 162, 165, 164,
)
STRIPE = 16


def shifted(position, by):
    return (position + by + SIDE) % SIDE


class Place:
    def __init__(self):
        self.row = lax.axis_index("row")
        self.col = lax.axis_index("col")
        self.z, self.core = self.row // 2, self.row % 2
        self.x, self.y = self.col // SIDE, self.col % SIDE

    def along(self, axis, by):
        if axis == 0:
            return (self.row, shifted(self.x, by) * SIDE + self.y)
        if axis == 1:
            return (self.row, self.x * SIDE + shifted(self.y, by))
        return (self.slot(by), self.col)

    def slot(self, by):
        return shifted(self.z, by) * 2 + self.core

    def partner(self):
        return (self.z * 2 + 1 - self.core, self.col)

    def greet(self, targets):
        barrier = pltpu.get_barrier_semaphore()
        for target in targets:
            pl.semaphore_signal(barrier, inc=1, device_id=target, device_id_type=MESH)
        pl.semaphore_wait(barrier, len(targets))


def remote(src, dst, send_sem, recv_sem, target):
    return pltpu.make_async_remote_copy(
        src_ref=src, dst_ref=dst, send_sem=send_sem, recv_sem=recv_sem, device_id=target, device_id_type=MESH
    )


class Parts:
    def __init__(self, sizes):
        self.sizes = sizes
        self.count = len(sizes)

    def low(self, group):
        return sum(self.sizes[:group])

    def near(self, group, half):
        size = self.sizes[group]
        first = size // 32 * 16 + size % 32
        return (self.low(group), first) if half == 0 else (self.low(group) + first, size - first)

    def rows(self, group):
        return pl.ds(self.low(group), self.sizes[group])

    def own(self, group, kind):
        return pl.ds(kind * HALF + self.low(group), self.sizes[group])

    def run(self, stages, order):
        for code in order:
            stages[code // 32](code % 32 // 2, code % 2)


def stripes(low, rows, body):
    @pl.loop(0, rows // STRIPE)
    def _(i):
        body(pl.multiple_of(low + i * STRIPE, STRIPE))


def wide(value):
    return value.astype(jnp.float32)


class Gather:
    def __init__(self, place, parts, panel, send_sem, recv_sem):
        self.place, self.parts, self.panel = place, parts, panel
        self.send_sem, self.recv_sem = send_sem, recv_sem

    def copy(self, group, kind, index):
        place = self.place
        rows = self.parts.own(group, kind)
        plus, minus, partner = place.along(2, 1), place.along(2, -1), place.partner()
        mine, below, above, far = place.slot(0), place.slot(-1), place.slot(1), place.slot(2)
        slot, target = [
            (mine, plus),
            (mine, minus),
            (mine, partner),
            (below, plus) if kind == 0 else (above, minus),
            (below, partner),
            (above, partner),
            (far, partner),
        ][index]
        block = self.panel.at[slot, rows]
        sems = (group, kind, index)
        return remote(block, block, self.send_sem.at[sems], self.recv_sem.at[sems], target)

    def neighbours(self):
        return [self.place.along(2, 1), self.place.along(2, -1), self.place.partner()]

    def first(self, group, kind):
        for index in range(3):
            self.copy(group, kind, index).start()

    def second(self, group, kind):
        self.copy(group, kind, kind).wait_recv()
        self.copy(group, kind, 3).start()
        self.copy(group, kind, 4 + kind).start()
        self.copy(group, kind, 1 - kind).wait_recv()
        self.copy(group, kind, 5 - kind).start()

    def third(self, group, kind):
        self.copy(group, kind, 3).wait_recv()
        self.copy(group, kind, 6).start()

    def close(self, group):
        for kind in range(2):
            for index in (2, 4, 5, 6):
                self.copy(group, kind, index).wait_recv()
            for index in range(7):
                self.copy(group, kind, index).wait_send()


def gather_kernel(start_ref, values_hbm, panel, values, load_sem, send_sem, recv_sem):
    place = Place()
    gather = Gather(place, Parts(GATHER_PARTS), panel, send_sem, recv_sem)
    load = pltpu.make_async_copy(start_ref, panel.at[place.slot(0)], load_sem.at[0])
    values_load = pltpu.make_async_copy(values_hbm, values, load_sem.at[1])
    load.start()
    place.greet(gather.neighbours())
    load.wait()
    for group in range(gather.parts.count):
        for kind in range(2):
            gather.first(group, kind)
        if group == 0:
            values_load.start()
    for group in range(gather.parts.count + 1):
        for kind in range(2):
            if group < gather.parts.count:
                gather.second(group, kind)
            if group > 0:
                gather.third(group - 1, kind)
    for group in range(gather.parts.count):
        gather.close(group)
    values_load.wait()


class Reduce:
    def __init__(self, place, parts, terms, sums, result, far_slots, near_slots, far_send, far_recv, near_send, near_recv):
        self.place, self.parts, self.terms = place, parts, terms
        self.sums, self.result, self.far_slots, self.near_slots = sums, result, far_slots, near_slots
        self.far_sems, self.near_sems = (far_send, far_recv), (near_send, near_recv)

    def position(self, axis):
        return self.place.x if axis == 0 else self.place.y

    def piece(self, kind, target, half, rows):
        span = pl.ds(2 * half, 2)
        return (target, span, rows) if kind == 0 else (span, target, rows)

    def far(self, group, kind, index):
        p = self.position(kind)
        rows, own = self.parts.rows(group), self.parts.own(group, kind)
        by = -1 if index in (RELAY_A, DIRECT_B, SUM_A) else 1
        if index in (RELAY_A, RELAY_B):
            source = self.terms.at[self.piece(kind, shifted(p, 2), index - RELAY_A, own)]
        elif index == DIRECT_A:
            source = self.terms.at[self.piece(kind, shifted(p, 1), 0, own)]
        elif index == DIRECT_B:
            source = self.terms.at[self.piece(kind, shifted(p, -1), 1, own)]
        else:
            source = self.sums.at[index - SUM_A, kind, :, rows]
        sems = (group, kind, index)
        return remote(
            source,
            self.far_slots.at[kind, index, :, rows],
            self.far_sems[0].at[sems],
            self.far_sems[1].at[sems],
            self.place.along(kind, by),
        )

    def near_copy(self, group, kind, index):
        axis = 1 - kind
        p = self.position(axis)
        half, by, to = {
            RELAY_A: (0, -1, 2),
            RELAY_B: (1, 1, 2),
            DIRECT_B: (1, -1, -1),
            DIRECT_A: (0, 1, 1),
            SUM_A: (0, -1, -1),
            SUM_B: (1, 1, 1),
        }[index]
        rows = pl.ds(*self.parts.near(group, half))
        sems = (group, kind, index)
        return remote(
            self.result.at[kind, shifted(p, to), rows],
            self.near_slots.at[kind, index // 2, rows],
            self.near_sems[0].at[sems],
            self.near_sems[1].at[sems],
            self.place.along(axis, by),
        )

    def neighbours(self):
        return [self.place.along(axis, by) for axis in (0, 1) for by in (1, -1)]

    def far_relays(self, group, kind):
        self.far(group, kind, RELAY_A).start()
        self.far(group, kind, RELAY_B).start()

    def far_directs(self, group, kind):
        self.far(group, kind, DIRECT_A).start()
        self.far(group, kind, DIRECT_B).start()

    def far_relay(self, group, kind):
        p = self.position(kind)
        for side, (arrived, leaving, to) in enumerate(((RELAY_A, SUM_A, -1), (RELAY_B, SUM_B, 1))):
            self.far(group, kind, arrived).wait_recv()
            target = shifted(p, to)

            def body(at, side=side, arrived=arrived, target=target):
                rows = pl.ds(at, STRIPE)
                own = pl.ds(kind * HALF + at, STRIPE)
                value = wide(self.terms[self.piece(kind, target, side, own)]) + wide(
                    self.far_slots[kind, arrived, :, rows]
                )
                self.sums[side, kind, :, rows] = value.astype(jnp.bfloat16)

            stripes(self.parts.low(group), self.parts.sizes[group], body)
            self.far(group, kind, leaving).start()

    def far_total(self, group, kind):
        p = self.position(kind)
        for index in (DIRECT_A, DIRECT_B, SUM_A, SUM_B):
            self.far(group, kind, index).wait_recv()

        def body(at):
            rows = pl.ds(at, STRIPE)
            own = pl.ds(kind * HALF + at, STRIPE)
            for half, (one, two) in enumerate(((DIRECT_A, SUM_A), (DIRECT_B, SUM_B))):
                value = (
                    wide(self.terms[self.piece(kind, p, half, own)])
                    + wide(self.far_slots[kind, one, :, rows])
                    + wide(self.far_slots[kind, two, :, rows])
                )
                self.result[kind, pl.ds(2 * half, 2), rows] = value.astype(jnp.bfloat16)

        stripes(self.parts.low(group), self.parts.sizes[group], body)
        for index in (RELAY_A, RELAY_B, DIRECT_A, DIRECT_B):
            self.near_copy(group, kind, index).start()

    def near_relay(self, group, kind):
        p = self.position(1 - kind)
        for half, (arrived, leaving, to) in enumerate(((RELAY_A, SUM_A, -1), (RELAY_B, SUM_B, 1))):
            self.near_copy(group, kind, arrived).wait_recv()
            target = shifted(p, to)

            def body(at, target=target):
                rows = pl.ds(at, STRIPE)
                value = wide(self.result[kind, target, rows]) + wide(self.near_slots[kind, 0, rows])
                self.result[kind, target, rows] = value.astype(jnp.bfloat16)

            stripes(*self.parts.near(group, half), body)
            self.near_copy(group, kind, leaving).start()

    def near_total(self, group, kind, finish):
        p = self.position(1 - kind)
        for half, (one, two) in enumerate(((DIRECT_A, SUM_A), (DIRECT_B, SUM_B))):
            self.near_copy(group, kind, one).wait_recv()
            self.near_copy(group, kind, two).wait_recv()

            def body(at):
                rows = pl.ds(at, STRIPE)
                value = (
                    wide(self.result[kind, p, rows])
                    + wide(self.near_slots[kind, 1, rows])
                    + wide(self.near_slots[kind, 2, rows])
                )
                finish(pl.ds(kind * HALF + at, STRIPE), value)

            stripes(*self.parts.near(group, half), body)

    def close(self, group):
        for kind in range(2):
            for index in range(6):
                self.far(group, kind, index).wait_send()
                self.near_copy(group, kind, index).wait_send()


def first_kernel(center, width, terms, source, panel, gather_send, gather_recv, *scratch):
    place = Place()
    parts = Parts(FIRST_PARTS)
    gather = Gather(place, parts, panel, gather_send, gather_recv)
    reduce = Reduce(place, parts, terms, *scratch)
    place.greet(reduce.neighbours() + gather.neighbours())
    mine = place.slot(0)

    def finish(rows, image):
        value = (image - center[0] * wide(source[rows])) / width[0]
        panel[mine, rows] = value.astype(jnp.bfloat16)

    def opened(group, kind):
        reduce.near_total(group, kind, finish)

    parts.run(
        [
            reduce.far_relays,
            reduce.far_directs,
            reduce.far_relay,
            reduce.far_total,
            reduce.near_relay,
            opened,
            gather.first,
            gather.second,
            gather.third,
        ],
        FIRST_ORDER,
    )
    for group in range(parts.count):
        reduce.close(group)
        gather.close(group)


def second_kernel(center, width, terms, source, panel, out, arriving, swap_sem, *scratch):
    place = Place()
    parts = Parts(SECOND_PARTS)
    reduce = Reduce(place, parts, terms, *scratch)
    place.greet(reduce.neighbours())
    parity = place.y % 2
    other = (place.row, place.x * SIDE + place.y + 1 - 2 * parity)
    mine = place.slot(0)

    def finish(rows, image):
        value = 2.0 * (image - center[0] * wide(panel[mine, rows])) / width[0] - wide(source[rows])
        out[rows] = value.astype(jnp.bfloat16)

    def swap(group):
        rows = pl.ds(pl.multiple_of((1 - parity) * HALF + parts.low(group), 16), parts.sizes[group])
        return remote(out.at[rows], arriving.at[parts.rows(group)], swap_sem.at[0, group], swap_sem.at[1, group], other)

    opened_halves = set()

    def opened(group, kind):
        reduce.near_total(group, kind, finish)
        opened_halves.add((group, kind))
        if (group, 1 - kind) in opened_halves:
            swap(group).start()

    parts.run(
        [
            reduce.far_relays,
            reduce.far_directs,
            reduce.far_relay,
            reduce.far_total,
            reduce.near_relay,
            opened,
        ],
        SECOND_ORDER,
    )
    for group in range(parts.count):
        reduce.close(group)
        swap(group).wait()


def reduce_scratch(count):
    bf16 = jnp.bfloat16
    dma = pltpu.SemaphoreType.DMA
    return [
        pltpu.VMEM((2, 2, 2, HALF, VECS), bf16),
        pltpu.VMEM((2, SIDE, HALF, VECS), bf16),
        pltpu.VMEM((2, 6, 2, HALF, VECS), bf16),
        pltpu.VMEM((2, 3, HALF, VECS), bf16),
        dma((count, 2, 6)),
        dma((count, 2, 6)),
        dma((count, 2, 6)),
        dma((count, 2, 6)),
    ]


HBM = pl.BlockSpec(memory_space=pltpu.HBM)
VMEM = pl.BlockSpec(memory_space=pltpu.VMEM)
SCALAR = pl.BlockSpec(memory_space=pltpu.SMEM)


def comm_call(kernel, name, collective_id, limit, in_specs, out_shape, scratch):
    return pl.pallas_call(
        kernel,
        out_shape=out_shape,
        in_specs=in_specs,
        out_specs=jax.tree.map(lambda _: VMEM, out_shape),
        scratch_shapes=scratch,
        compiler_params=pltpu.CompilerParams(
            collective_id=collective_id, has_side_effects=True, vmem_limit_bytes=limit * 1024 * 1024
        ),
        name=name,
    )


def panel_shape(row_count):
    return jax.ShapeDtypeStruct((row_count, ROWS, VECS), jnp.bfloat16)


def gather_scratch(count):
    dma = pltpu.SemaphoreType.DMA
    return [dma((count, 2, 7)), dma((count, 2, 7))]


def gathered(start, values, row_count):
    return comm_call(
        gather_kernel,
        "gather_rows",
        0,
        LIMITS[0],
        [HBM, HBM],
        (panel_shape(row_count), jax.ShapeDtypeStruct(values.shape, values.dtype)),
        [pltpu.SemaphoreType.DMA((2,))] + gather_scratch(len(GATHER_PARTS)),
    )(start, values)


def first_of(center, width, terms, start, row_count):
    count = len(FIRST_PARTS)
    return comm_call(
        first_kernel,
        "reduce_and_gather",
        1,
        LIMITS[1],
        [SCALAR, SCALAR, VMEM, VMEM],
        panel_shape(row_count),
        gather_scratch(count) + reduce_scratch(count),
    )(center, width, terms.reshape(SIDE, SIDE, ROWS, VECS), start)


def second_of(center, width, terms, start, panel):
    count = len(SECOND_PARTS)
    return comm_call(
        second_kernel,
        "reduce_and_swap",
        2,
        LIMITS[2],
        [SCALAR, SCALAR, VMEM, VMEM, VMEM],
        (
            jax.ShapeDtypeStruct((ROWS, VECS), jnp.bfloat16),
            jax.ShapeDtypeStruct((HALF, VECS), jnp.bfloat16),
        ),
        [pltpu.SemaphoreType.DMA((2, count))] + reduce_scratch(count),
    )(center, width, terms.reshape(SIDE, SIDE, ROWS, VECS), start, panel)


LIMITS = (4, 22, 22)


def on_device(block_values, block_rows, block_cols, start_vectors, center, half_width, row_counts):
    values = block_values.reshape(-1, ORB, ORB)
    codes = entry_codes(block_rows.reshape(-1), block_cols.reshape(-1))
    col_count = lax.axis_size("col")
    row_count = lax.axis_size("row")
    out_blocks = col_count * BD

    panel, values = gathered(
        pltpu.with_memory_space_constraint(start_vectors, pltpu.HBM),
        pltpu.with_memory_space_constraint(values, pltpu.HBM),
        row_count,
    )
    terms = cell_terms(codes, values, panel, out_blocks)
    panel = first_of(center, half_width, terms, start_vectors, row_count)
    terms = cell_terms(codes, values, panel, out_blocks)
    second, arriving = second_of(center, half_width, terms, start_vectors, panel)

    device = lax.axis_index("row") * col_count + lax.axis_index("col")
    parity = device % 2
    even_count = row_counts[device - parity]
    own_count = row_counts[device]
    start_row = jnp.where(parity == 0, 0, even_count * ORB - HALF)
    capacity = (BD + MOVE) * ORB
    window = jnp.where(
        parity == 0, jnp.concatenate([second, arriving], 0), jnp.concatenate([arriving, second], 0)
    )
    padded = jnp.concatenate([window, jnp.zeros((capacity, VECS), jnp.bfloat16)], 0)
    selected = lax.dynamic_slice_in_dim(padded, start_row, capacity, 0)
    live_rows = jnp.arange(capacity, dtype=jnp.int32)[:, None] < own_count * ORB
    return jnp.where(live_rows, selected, jnp.zeros_like(selected))


def solution(mesh):
    placed = (
        P("row", "col", None, None, None),
        P("row", "col", None),
        P("row", "col", None),
        P(("row", "col"), None),
        P(),
        P(),
        P(),
    )
    return jax.shard_map(
        on_device, mesh=mesh, in_specs=placed, out_specs=P(("row", "col"), None), check_vma=False
    )
```

time: 647 us -> 244 us (0.38)
  waiting for transfers between devices: 297 us -> 0 us
  Pallas kernels: 0 us -> 234 us
  other arithmetic: 200 us -> 4.47 us
  local copies, waits for them, and re-layouts: 71.9 us -> 1.4 us
  matrix products: 58.4 us -> 0 us
  between operations: 15.8 us -> 2.72 us
    pallas_call x0 -> x5, Pallas kernels: none -> 234 us  [the longest x1 93.1 us: first_of(): comm_call(first_kernel, 'reduce_and_gather', 1, LIMITS[1], [SCALAR, SCALA...]
    reduce_scatter x2 -> x0, waiting for transfers between devices: 193 us -> none  [image_of(): lax.psum_scatter(cell_terms.astype(jnp.bfloat16), 'col', scatter_dimensio...]
    scatter-add x8 -> x0, other arithmetic: 158 us -> none  [add_group(): return (row_images.at[group_rows].add(images), None)]
    all_gather x2 -> x0, waiting for transfers between devices: 87 us -> none  [image_of(): panel_rows = lax.all_gather(vectors, 'row', axis=0, tiled=True)]
    dot_general x8 -> x0, matrix products: 58.4 us -> none  [add_group(): jnp.einsum('gij,gjv->giv', group_values, picked, preferred_element_type=j...]
    gather x8 -> x0, local copies, waits for them, and re-layouts: 45.7 us -> none  [add_group(): picked = blocks[group_cols]]
    convert_element_type x4 -> x0, other arithmetic: 35.3 us -> none  [the longest x2 31.1 us: image_of(): cell_terms.astype(jnp.bfloat16)]
    another operation x4 -> x0, local copies, waits for them, and re-layouts: 25.1 us -> none
  transfers between devices with their start and end apart: 5 -> 0, of which waited for: 5 -> 0; matrix products, arithmetic and copies ran while one was open for 1% -> 0% of each run, Pallas kernels for 0% -> 0%
where the time goes in v3:
time: 244 us; the launch traced here: 243 us
  Pallas kernels  234 us (96%)
  other arithmetic  4.47 us (2%)
  between operations  2.72 us (1%)
    pallas_call x1, Pallas kernels, first_of(): comm_call(first_kernel, 'reduce_and_gather', 1, LIMITS[1], [SCALAR, SCALA...  93.1 us
    pallas_call x1, Pallas kernels, second_of(): comm_call(second_kernel, 'reduce_and_swap', 2, LIMITS[2], [SCALAR, SCALAR...  82.7 us
    pallas_call x1, Pallas kernels, gathered(): comm_call(gather_kernel, 'gather_rows', 0, LIMITS[0], [HBM, HBM], (panel_...  36 us
    pallas_call x2, Pallas kernels, cell_terms(): pl.pallas_call(product_kernel, out_shape=jax.ShapeDtypeStruct((out_blocks...  22.2 us

profile of v3, /device:TPU:8, one launch (start us, length us, event | category | flops | bytes accessed | tf_op | source)
XLA Modules:
  0.0 242.6 jit_solution(16385676495257681456)
XLA Ops:
  0.0 1.4 fusion.1
  3.4 0.7 add_multiply_fusion
  4.1 0.2 convert_reduce_fusion
  4.3 0.2 select_reduce_fusion.codes_ref
  4.4 36.0 %gather_rows.1 = (bf16[8,1664,256]{2,1,0:T(8,128)(2,1)S(1)}, bf16[256,128,128]{2,1,0:T(8,128)(2,1)S(1)}) custom-call(bf16[1664,256]{1,0:T(8,128)(2,1)} %source.3, bf16[256,128,128]{2,1,0:T(8,128)(2,1)} %bitcast.12), custom_call_target="tpu_custom_call" | custom-call | tf_op jit(solution)/shard_map/gather_rows/pallas_call | solution.py:488
  40.4 0.0 copy-start
  40.4 11.1 %block_products.2 = bf16[208,128,256]{2,1,0:T(8,128)(2,1)S(1)} custom-call(s32[256]{0:T(256)S(1)} %select_reduce_fusion.codes_ref, bf16[256,128,128]{2,1,0:T(8,128)(2,1)S(1)} %get-tuple-element.9.values_ref, bf16[104,128,256]{2,1,0:T(8,128)(2,1)S(1)} %bitcast.11), custom_call_target="tpu_custom_call" | custom-call | tf_op jit(solution)/shard_map/block_products/pallas_call | solution.py:49
  51.6 0.0 copy-done
  51.6 93.1 %reduce_and_gather.1.panel = bf16[8,1664,256]{2,1,0:T(8,128)(2,1)S(1)} custom-call(f32[1]{0:T(128)S(6)} %copy.8.center, f32[1]{0:T(128)S(6)} %copy.9.width, bf16[4,4,1664,256]{3,2,1,0:T(8,128)(2,1)S(1)} %bitcast.10, bf16[1664,256]{1,0:T(8,128)(2,1)S(1)} %copy-done), custom_call_target="tpu_custom_call" | custom-call | tf_op jit(solution)/shard_map/reduce_and_gather/pallas_call | solution.py:501
  144.7 11.1 %block_products.3 = bf16[208,128,256]{2,1,0:T(8,128)(2,1)S(1)} custom-call(s32[256]{0:T(256)S(1)} %select_reduce_fusion.codes_ref, bf16[256,128,128]{2,1,0:T(8,128)(2,1)S(1)} %get-tuple-element.9.values_ref, bf16[104,128,256]{2,1,0:T(8,128)(2,1)S(1)} %bitcast.8), custom_call_target="tpu_custom_call" | custom-call | tf_op jit(solution)/shard_map/block_products/pallas_call | solution.py:49
  155.8 82.7 %reduce_and_swap.1 = (bf16[1664,256]{1,0:T(8,128)(2,1)S(1)}, bf16[832,256]{1,0:T(8,128)(2,1)S(1)}) custom-call(f32[1]{0:T(128)S(6)} %copy.8.center, f32[1]{0:T(128)S(6)} %copy.9.width, bf16[4,4,1664,256]{3,2,1,0:T(8,128)(2,1)S(1)} %bitcast.9, bf16[1664,256]{1,0:T(8,128)(2,1)S(1)} %copy-done, bf16[8,1664,256]{2,1,0:T(8,128)(2,1)S(1)} %reduce_and_gather.1.panel), custom_call_target="tpu_custom_call" | custom-call | tf_op jit(solution)/shard_map/reduce_and_swap/pallas_call | solution.py:514
  238.6 0.3 maximum_select_fusion
  239.5 3.1 %fusion = bf16[2432,256]{1,0:T(8,128)(2,1)} fusion(s32[]{:T(128)S(6)} %select_n.43, bf16[2496,256]{1,0:T(8,128)(2,1)S(1)} %maximum_select_fusion, pred[2432]{0:T(1024)(128)(4,1)S(1)} %iota_compare_fusion.1), kind=kLoop, calls=%fused_computation.2 | loop fusion | flops 622592 | bytes 2525572 | tf_op jit(solution)/shard_map/jit(_where)/select_n | solution.py:560
  (2 shorter events, 0.0 us)
Async XLA Ops:
  40.4 11.2 %copy-start = (bf16[1664,256]{1,0:T(8,128)(2,1)S(1)}, bf16[1664,256]{1,0:T(8,128)(2,1)}, u32[]{:S(2)}) copy-start(bf16[1664,256]{1,0:T(8,128)(2,1)} %source.3) | copy-start | bytes 2555908

commit v4 on v3

--- a/solution.py
+++ b/solution.py
@@ -11,7 +11,7 @@
 VECS = 256
 BD = 13
 MOVE = 6
-GROUP = 8
+GROUP = 64
 
 
 def product_kernel(codes_ref, values_ref, panel_ref, out_ref):
@@ -22,7 +22,7 @@
     def group(step, carry):
         before, total = carry
         for e in range(GROUP):
-            code = codes_ref[step * GROUP + e]
+            code = codes_ref[0, step * GROUP + e]
             row, col, entry = code >> 15, (code >> 8) & 127, code & 255
             product = jnp.dot(values_ref[entry], panel_ref[col], preferred_element_type=jnp.float32)
             total = jnp.where(row == before, total, 0.0) + product
@@ -33,14 +33,6 @@
     lax.fori_loop(
         0, values_ref.shape[0] // GROUP, group, (jnp.int32(-1), jnp.zeros((ORB, VECS), jnp.float32))
     )
-
-
-def entry_codes(row_ids, col_ids):
-    count = row_ids.shape[0]
-    codes = (row_ids * 128 + col_ids) * 256 + jnp.arange(count, dtype=jnp.int32)
-    rank = jnp.sum((codes[None, :] < codes[:, None]).astype(jnp.int32), 1)
-    here = rank[:, None] == jnp.arange(count, dtype=jnp.int32)[None, :]
-    return jnp.sum(jnp.where(here, codes[:, None], 0), 0)
 
 
 def cell_terms(codes, values, panel_rows, out_blocks):
@@ -62,23 +54,20 @@
 HALF = BD * ORB // 2
 ROWS = BD * ORB
 GATHER_PARTS = (416, 416)
-FIRST_PARTS = (160, 176, 144, 112, 96, 80, 64)
-SECOND_PARTS = (208, 352, 272)
+FIRST_PARTS = (256, 256, 192, 128)
+SECOND_PARTS = (448, 384)
 RELAY_A, RELAY_B, DIRECT_A, DIRECT_B, SUM_A, SUM_B = range(6)
 FIRST_ORDER = (
     0, 1, 32, 33, 2, 3, 64, 65, 34, 35, 66, 67, 96, 97, 4, 5, 98, 128, 129, 99,
-    36, 37, 68, 161, 193, 130, 131, 160, 192, 69, 225, 6, 7, 224, 162, 194, 38, 39, 257, 100,
-    256, 163, 195, 226, 101, 70, 71, 227, 8, 9, 133, 132, 258, 40, 41, 259, 102, 103, 72, 164,
-    196, 165, 197, 73, 10, 135, 134, 228, 11, 42, 43, 12, 229, 13, 104, 166, 198, 260, 105, 261,
-    167, 199, 74, 230, 75, 44, 45, 76, 231, 136, 137, 77, 262, 106, 263, 107, 168, 200, 108, 169,
-    201, 138, 139, 109, 232, 140, 170, 202, 233, 171, 203, 141, 172, 204, 264, 234, 173, 205, 265, 235,
-    236, 266, 237, 267, 268, 269,
+    36, 37, 68, 69, 161, 193, 130, 131, 160, 192, 225, 6, 7, 224, 38, 39, 257, 100, 256, 101,
+    162, 194, 163, 195, 70, 71, 226, 133, 132, 227, 102, 103, 258, 164, 196, 259, 165, 197, 134, 135,
+    166, 198, 228, 167, 199, 229, 230, 260, 231, 261, 262, 263,
 )
 SECOND_ORDER = (
-    0, 1, 32, 33, 2, 3, 34, 35, 64, 65, 4, 5, 66, 67, 96, 97, 36, 37, 68, 69,
-    98, 128, 129, 99, 100, 161, 130, 131, 160, 101, 163, 132, 133, 162, 165, 164,
+    0, 1, 32, 33, 2, 3, 64, 65, 34, 35, 66, 67, 96, 97, 98, 99, 128, 129, 130, 131,
+    160, 161, 162, 163,
 )
-STRIPE = 16
+STRIPE = 32
 
 
 def shifted(position, by):
@@ -153,8 +142,8 @@
 
 
 class Gather:
-    def __init__(self, place, parts, panel, send_sem, recv_sem):
-        self.place, self.parts, self.panel = place, parts, panel
+    def __init__(self, place, parts, panel, send_sem, recv_sem, own=None):
+        self.place, self.parts, self.panel, self.own = place, parts, panel, own
         self.send_sem, self.recv_sem = send_sem, recv_sem
 
     def copy(self, group, kind, index):
@@ -173,7 +162,8 @@
         ][index]
         block = self.panel.at[slot, rows]
         sems = (group, kind, index)
-        return remote(block, block, self.send_sem.at[sems], self.recv_sem.at[sems], target)
+        source = self.own.at[rows] if self.own is not None and index < 3 else block
+        return remote(source, block, self.send_sem.at[sems], self.recv_sem.at[sems], target)
 
     def neighbours(self):
         return [self.place.along(2, 1), self.place.along(2, -1), self.place.partner()]
@@ -201,19 +191,29 @@
                 self.copy(group, kind, index).wait_send()
 
 
-def gather_kernel(start_ref, values_hbm, panel, values, load_sem, send_sem, recv_sem):
+def sorted_codes(rows_ref, cols_ref):
+    count = rows_ref.shape[1]
+    entry = lax.broadcasted_iota(jnp.int32, (1, count), 1)
+    codes = wide((rows_ref[...] * 128 + cols_ref[...]) * 256 + entry)
+    across = jnp.broadcast_to(codes, (count, count))
+    down = across.T
+    rank = jnp.sum(jnp.where(across < down, 1.0, 0.0), axis=1, keepdims=True)
+    place = wide(lax.broadcasted_iota(jnp.int32, (count, count), 1))
+    return jnp.sum(jnp.where(rank == place, down, 0.0), axis=0, keepdims=True).astype(jnp.int32)
+
+
+def gather_kernel(rows_ref, cols_ref, start_hbm, values_hbm, panel, values, codes, load_sem, send_sem, recv_sem):
     place = Place()
-    gather = Gather(place, Parts(GATHER_PARTS), panel, send_sem, recv_sem)
-    load = pltpu.make_async_copy(start_ref, panel.at[place.slot(0)], load_sem.at[0])
+    gather = Gather(place, Parts(GATHER_PARTS), panel, send_sem, recv_sem, start_hbm)
+    load = pltpu.make_async_copy(start_hbm, panel.at[place.slot(0)], load_sem.at[0])
     values_load = pltpu.make_async_copy(values_hbm, values, load_sem.at[1])
-    load.start()
     place.greet(gather.neighbours())
-    load.wait()
     for group in range(gather.parts.count):
         for kind in range(2):
             gather.first(group, kind)
-        if group == 0:
-            values_load.start()
+    load.start()
+    values_load.start()
+    codes[...] = sorted_codes(rows_ref, cols_ref)
     for group in range(gather.parts.count + 1):
         for kind in range(2):
             if group < gather.parts.count:
@@ -222,6 +222,7 @@
                 gather.third(group - 1, kind)
     for group in range(gather.parts.count):
         gather.close(group)
+    load.wait()
     values_load.wait()
 
 
@@ -300,10 +301,9 @@
             def body(at, side=side, arrived=arrived, target=target):
                 rows = pl.ds(at, STRIPE)
                 own = pl.ds(kind * HALF + at, STRIPE)
-                value = wide(self.terms[self.piece(kind, target, side, own)]) + wide(
-                    self.far_slots[kind, arrived, :, rows]
+                self.sums[side, kind, :, rows] = (
+                    self.terms[self.piece(kind, target, side, own)] + self.far_slots[kind, arrived, :, rows]
                 )
-                self.sums[side, kind, :, rows] = value.astype(jnp.bfloat16)
 
             stripes(self.parts.low(group), self.parts.sizes[group], body)
             self.far(group, kind, leaving).start()
@@ -336,8 +336,7 @@
 
             def body(at, target=target):
                 rows = pl.ds(at, STRIPE)
-                value = wide(self.result[kind, target, rows]) + wide(self.near_slots[kind, 0, rows])
-                self.result[kind, target, rows] = value.astype(jnp.bfloat16)
+                self.result[kind, target, rows] += self.near_slots[kind, 0, rows]
 
             stripes(*self.parts.near(group, half), body)
             self.near_copy(group, kind, leaving).start()
@@ -484,16 +483,20 @@
     return [dma((count, 2, 7)), dma((count, 2, 7))]
 
 
-def gathered(start, values, row_count):
+def gathered(row_ids, col_ids, start, values, row_count):
     return comm_call(
         gather_kernel,
         "gather_rows",
         0,
         LIMITS[0],
-        [HBM, HBM],
-        (panel_shape(row_count), jax.ShapeDtypeStruct(values.shape, values.dtype)),
+        [VMEM, VMEM, HBM, HBM],
+        (
+            panel_shape(row_count),
+            jax.ShapeDtypeStruct(values.shape, values.dtype),
+            jax.ShapeDtypeStruct(row_ids.shape, jnp.int32),
+        ),
         [pltpu.SemaphoreType.DMA((2,))] + gather_scratch(len(GATHER_PARTS)),
-    )(start, values)
+    )(row_ids, col_ids, start, values)
 
 
 def first_of(center, width, terms, start, row_count):
@@ -530,12 +533,15 @@
 
 def on_device(block_values, block_rows, block_cols, start_vectors, center, half_width, row_counts):
     values = block_values.reshape(-1, ORB, ORB)
-    codes = entry_codes(block_rows.reshape(-1), block_cols.reshape(-1))
+    row_ids = block_rows.reshape(1, -1)
+    col_ids = block_cols.reshape(1, -1)
     col_count = lax.axis_size("col")
     row_count = lax.axis_size("row")
     out_blocks = col_count * BD
 
-    panel, values = gathered(
+    panel, values, codes = gathered(
+        row_ids,
+        col_ids,
         pltpu.with_memory_space_constraint(start_vectors, pltpu.HBM),
         pltpu.with_memory_space_constraint(values, pltpu.HBM),
         row_count,
@@ -545,19 +551,50 @@
     terms = cell_terms(codes, values, panel, out_blocks)
     second, arriving = second_of(center, half_width, terms, start_vectors, panel)
 
-    device = lax.axis_index("row") * col_count + lax.axis_index("col")
+    return placed_rows(row_counts, second, arriving)
+
+
+UNIT = ORB // 2
+
+
+def placing_kernel(counts_ref, second, arriving, out):
+    device = lax.axis_index("row") * lax.axis_size("col") + lax.axis_index("col")
     parity = device % 2
-    even_count = row_counts[device - parity]
-    own_count = row_counts[device]
-    start_row = jnp.where(parity == 0, 0, even_count * ORB - HALF)
-    capacity = (BD + MOVE) * ORB
-    window = jnp.where(
-        parity == 0, jnp.concatenate([second, arriving], 0), jnp.concatenate([arriving, second], 0)
-    )
-    padded = jnp.concatenate([window, jnp.zeros((capacity, VECS), jnp.bfloat16)], 0)
-    selected = lax.dynamic_slice_in_dim(padded, start_row, capacity, 0)
-    live_rows = jnp.arange(capacity, dtype=jnp.int32)[:, None] < own_count * ORB
-    return jnp.where(live_rows, selected, jnp.zeros_like(selected))
+    even_count = counts_ref[device - parity]
+    live = 2 * counts_ref[device]
+    first = parity * (2 * even_count - BD)
+
+    @pl.loop(0, out.shape[0] // UNIT)
+    def _(unit):
+        at = first + unit
+        here = pl.ds(pl.multiple_of(unit * UNIT, UNIT), UNIT)
+        own_at = at - parity * BD
+        other_at = at - (1 - parity) * 2 * BD
+        is_own = jnp.logical_and(own_at >= 0, own_at < 2 * BD)
+        is_live = unit < live
+
+        @pl.when(jnp.logical_and(is_live, is_own))
+        def _():
+            out[here] = second[pl.ds(pl.multiple_of(own_at * UNIT, UNIT), UNIT)]
+
+        @pl.when(jnp.logical_and(is_live, jnp.logical_not(is_own)))
+        def _():
+            out[here] = arriving[pl.ds(pl.multiple_of(other_at * UNIT, UNIT), UNIT)]
+
+        @pl.when(jnp.logical_not(is_live))
+        def _():
+            out[here] = jnp.zeros((UNIT, VECS), jnp.bfloat16)
+
+
+def placed_rows(row_counts, second, arriving):
+    return pl.pallas_call(
+        placing_kernel,
+        out_shape=jax.ShapeDtypeStruct(((BD + MOVE) * ORB, VECS), jnp.bfloat16),
+        in_specs=[SCALAR, VMEM, VMEM],
+        out_specs=VMEM,
+        compiler_params=pltpu.CompilerParams(vmem_limit_bytes=10 * 1024 * 1024),
+        name="place_rows",
+    )(row_counts, second, arriving)
 
 
 def solution(mesh):

time: 244 us -> 229 us (0.939)
  Pallas kernels: 234 us -> 226 us
  other arithmetic: 4.47 us -> 0 us
    pallas_call x2, Pallas kernels: 22.2 us -> 13.5 us  [cell_terms(): pl.pallas_call(product_kernel, out_shape=jax.ShapeDtypeStruct((out_blocks...]
    select_n x2 -> x0, other arithmetic: 3.42 us -> none  [the longest x1 3.13 us: on_device(): return jnp.where(live_rows, selected, jnp.zeros_like(selected))]
    pallas_call x1 -> x2, Pallas kernels: 36 us -> 38.5 us  [the longest x1 36.1 us: gathered(): comm_call(gather_kernel, 'gather_rows', 0, LIMITS[0], [VMEM, VMEM, HBM, H...]
where the time goes in v4:
time: 229 us
  Pallas kernels  226 us (99%)
    pallas_call x1, Pallas kernels, first_of(): comm_call(first_kernel, 'reduce_and_gather', 1, LIMITS[1], [SCALAR, SCALA...  90.7 us
    pallas_call x1, Pallas kernels, second_of(): comm_call(second_kernel, 'reduce_and_swap', 2, LIMITS[2], [SCALAR, SCALAR...  83.3 us
    pallas_call x1, Pallas kernels, gathered(): comm_call(gather_kernel, 'gather_rows', 0, LIMITS[0], [VMEM, VMEM, HBM, H...  36.1 us
    pallas_call x2, Pallas kernels, cell_terms(): pl.pallas_call(product_kernel, out_shape=jax.ShapeDtypeStruct((out_blocks...  13.5 us

profile of v4, /device:TPU:8, one launch (start us, length us, event | category | flops | bytes accessed | tf_op | source)
XLA Modules:
  0.0 228.8 jit_solution(8540582319711823740)
XLA Ops:
  1.3 0.0 copy-start.1
  1.3 0.7 copy-done.1
  2.0 0.0 copy-start.2
  2.0 0.7 copy-done.2
  2.7 36.1 %gather_rows.1 = (bf16[8,1664,256]{2,1,0:T(8,128)(2,1)S(1)}, bf16[256,128,128]{2,1,0:T(8,128)(2,1)S(1)}, s32[1,256]{1,0:T(1,128)S(1)}) custom-call(s32[1,256]{1,0:T(1,128)S(1)} %bitcast.11, s32[1,256]{1,0:T(1,128)S(1)} %bitcast.12, bf16[1664,256]{1,0:T(8,128)(2,1)} %source.3, bf16[256,128,128]{2,1,0:T(8,128)(2,1)} %bitcast.13), custom_call_target="tpu_custom_call" | custom-call | tf_op jit(solution)/shard_map/gather_rows/pallas_call | solution.py:487
  38.7 0.0 copy-start
  38.7 6.8 %block_products.2 = bf16[208,128,256]{2,1,0:T(8,128)(2,1)S(1)} custom-call(s32[1,256]{1,0:T(1,128)S(1)} %get-tuple-element.10.codes_ref, bf16[256,128,128]{2,1,0:T(8,128)(2,1)S(1)} %get-tuple-element.11.values_ref, bf16[104,128,256]{2,1,0:T(8,128)(2,1)S(1)} %bitcast.10), custom_call_target="tpu_custom_call" | custom-call | tf_op jit(solution)/shard_map/block_products/pallas_call | solution.py:41
  45.5 0.0 copy-done
  45.5 90.7 %reduce_and_gather.1.panel = bf16[8,1664,256]{2,1,0:T(8,128)(2,1)S(1)} custom-call(f32[1]{0:T(128)S(6)} %copy.8.center, f32[1]{0:T(128)S(6)} %copy.9.width, bf16[4,4,1664,256]{3,2,1,0:T(8,128)(2,1)S(1)} %bitcast.9, bf16[1664,256]{1,0:T(8,128)(2,1)S(1)} %copy-done), custom_call_target="tpu_custom_call" | custom-call | tf_op jit(solution)/shard_map/reduce_and_gather/pallas_call | solution.py:504
  136.3 6.8 %block_products.3 = bf16[208,128,256]{2,1,0:T(8,128)(2,1)S(1)} custom-call(s32[1,256]{1,0:T(1,128)S(1)} %get-tuple-element.10.codes_ref, bf16[256,128,128]{2,1,0:T(8,128)(2,1)S(1)} %get-tuple-element.11.values_ref, bf16[104,128,256]{2,1,0:T(8,128)(2,1)S(1)} %bitcast.7), custom_call_target="tpu_custom_call" | custom-call | tf_op jit(solution)/shard_map/block_products/pallas_call | solution.py:41
  143.0 0.0 copy-start.3
  143.0 83.3 %reduce_and_swap.1 = (bf16[1664,256]{1,0:T(8,128)(2,1)S(1)}, bf16[832,256]{1,0:T(8,128)(2,1)S(1)}) custom-call(f32[1]{0:T(128)S(6)} %copy.8.center, f32[1]{0:T(128)S(6)} %copy.9.width, bf16[4,4,1664,256]{3,2,1,0:T(8,128)(2,1)S(1)} %bitcast.8, bf16[1664,256]{1,0:T(8,128)(2,1)S(1)} %copy-done, bf16[8,1664,256]{2,1,0:T(8,128)(2,1)S(1)} %reduce_and_gather.1.panel), custom_call_target="tpu_custom_call" | custom-call | tf_op jit(solution)/shard_map/reduce_and_swap/pallas_call | solution.py:517
  226.3 0.0 copy-done.3
  226.3 2.5 %place_rows.1 = bf16[2432,256]{1,0:T(8,128)(2,1)} custom-call(s32[128]{0:T(128)S(1)} %copy-done.3, bf16[1664,256]{1,0:T(8,128)(2,1)S(1)} %get-tuple-element.13.second, bf16[832,256]{1,0:T(8,128)(2,1)S(1)} %get-tuple-element.14.arriving), custom_call_target="tpu_custom_call" | custom-call | tf_op jit(solution)/shard_map/place_rows/pallas_call | solution.py:590
Async XLA Ops:
  1.3 0.7 copy-start.1
  2.0 0.7 copy-start.2
  38.7 6.8 %copy-start = (bf16[1664,256]{1,0:T(8,128)(2,1)S(1)}, bf16[1664,256]{1,0:T(8,128)(2,1)}, u32[]{:S(2)}) copy-start(bf16[1664,256]{1,0:T(8,128)(2,1)} %source.3) | copy-start | bytes 2555908
  143.0 83.3 %copy-start.3 = (s32[128]{0:T(128)S(1)}, s32[128]{0:T(128)}, u32[]{:S(2)}) copy-start(s32[128]{0:T(128)} %counts_ref.1) | copy-start | bytes 1540

commit v5 on v4

--- a/solution.py
+++ b/solution.py
@@ -53,7 +53,7 @@
 SIDE = 4
 HALF = BD * ORB // 2
 ROWS = BD * ORB
-GATHER_PARTS = (416, 416)
+GATHER_PARTS = (832,)
 FIRST_PARTS = (256, 256, 192, 128)
 SECOND_PARTS = (448, 384)
 RELAY_A, RELAY_B, DIRECT_A, DIRECT_B, SUM_A, SUM_B = range(6)
@@ -202,17 +202,25 @@
     return jnp.sum(jnp.where(rank == place, down, 0.0), axis=0, keepdims=True).astype(jnp.int32)
 
 
-def gather_kernel(rows_ref, cols_ref, start_hbm, values_hbm, panel, values, codes, load_sem, send_sem, recv_sem):
+def gather_kernel(rows_hbm, cols_hbm, start_hbm, values_hbm, panel, values, codes, rows_ref, cols_ref, load_sem, send_sem, recv_sem):
     place = Place()
     gather = Gather(place, Parts(GATHER_PARTS), panel, send_sem, recv_sem, start_hbm)
     load = pltpu.make_async_copy(start_hbm, panel.at[place.slot(0)], load_sem.at[0])
     values_load = pltpu.make_async_copy(values_hbm, values, load_sem.at[1])
+    id_loads = [
+        pltpu.make_async_copy(rows_hbm, rows_ref, load_sem.at[2]),
+        pltpu.make_async_copy(cols_hbm, cols_ref, load_sem.at[3]),
+    ]
+    for id_load in id_loads:
+        id_load.start()
     place.greet(gather.neighbours())
     for group in range(gather.parts.count):
         for kind in range(2):
             gather.first(group, kind)
     load.start()
     values_load.start()
+    for id_load in id_loads:
+        id_load.wait()
     codes[...] = sorted_codes(rows_ref, cols_ref)
     for group in range(gather.parts.count + 1):
         for kind in range(2):
@@ -489,14 +497,16 @@
         "gather_rows",
         0,
         LIMITS[0],
-        [VMEM, VMEM, HBM, HBM],
+        [HBM, HBM, HBM, HBM],
         (
             panel_shape(row_count),
             jax.ShapeDtypeStruct(values.shape, values.dtype),
             jax.ShapeDtypeStruct(row_ids.shape, jnp.int32),
         ),
-        [pltpu.SemaphoreType.DMA((2,))] + gather_scratch(len(GATHER_PARTS)),
-    )(row_ids, col_ids, start, values)
+        [pltpu.VMEM(row_ids.shape, jnp.int32)] * 2
+        + [pltpu.SemaphoreType.DMA((4,))]
+        + gather_scratch(len(GATHER_PARTS)),
+    )(*[pltpu.with_memory_space_constraint(value, pltpu.HBM) for value in (row_ids, col_ids, start, values)])
 
 
 def first_of(center, width, terms, start, row_count):
@@ -539,13 +549,7 @@
     row_count = lax.axis_size("row")
     out_blocks = col_count * BD
 
-    panel, values, codes = gathered(
-        row_ids,
-        col_ids,
-        pltpu.with_memory_space_constraint(start_vectors, pltpu.HBM),
-        pltpu.with_memory_space_constraint(values, pltpu.HBM),
-        row_count,
-    )
+    panel, values, codes = gathered(row_ids, col_ids, start_vectors, values, row_count)
     terms = cell_terms(codes, values, panel, out_blocks)
     panel = first_of(center, half_width, terms, start_vectors, row_count)
     terms = cell_terms(codes, values, panel, out_blocks)

time: 229 us -> 227 us (level)
  no operation moved by 1% of the time
where the time goes in v5:
time: 227 us
  Pallas kernels  225 us (99%)
    pallas_call x1, Pallas kernels, first_of(): comm_call(first_kernel, 'reduce_and_gather', 1, LIMITS[1], [SCALAR, SCALA...  90.7 us
    pallas_call x1, Pallas kernels, second_of(): comm_call(second_kernel, 'reduce_and_swap', 2, LIMITS[2], [SCALAR, SCALAR...  83.2 us
    pallas_call x1, Pallas kernels, gathered(): comm_call(gather_kernel, 'gather_rows', 0, LIMITS[0], [HBM, HBM, HBM, HBM...  35.4 us
    pallas_call x2, Pallas kernels, cell_terms(): pl.pallas_call(product_kernel, out_shape=jax.ShapeDtypeStruct((out_blocks...  13.5 us

profile of v5, /device:TPU:8, one launch (start us, length us, event | category | flops | bytes accessed | tf_op | source)
XLA Modules:
  0.0 226.7 jit_solution(10132472027413116333)
XLA Ops:
  1.3 35.4 %gather_rows.1 = (bf16[8,1664,256]{2,1,0:T(8,128)(2,1)S(1)}, bf16[256,128,128]{2,1,0:T(8,128)(2,1)S(1)}, s32[1,256]{1,0:T(1,128)S(1)}) custom-call(s32[1,256]{1,0:T(1,128)} %bitcast.12, s32[1,256]{1,0:T(1,128)} %bitcast.13, bf16[1664,256]{1,0:T(8,128)(2,1)} %source.3, bf16[256,128,128]{2,1,0:T(8,128)(2,1)} %bitcast.11), custom_call_target="tpu_custom_call" | custom-call | tf_op jit(solution)/shard_map/gather_rows/pallas_call | solution.py:495
  36.7 0.0 copy-start
  36.7 6.8 %block_products.2 = bf16[208,128,256]{2,1,0:T(8,128)(2,1)S(1)} custom-call(s32[1,256]{1,0:T(1,128)S(1)} %get-tuple-element.10.codes_ref, bf16[256,128,128]{2,1,0:T(8,128)(2,1)S(1)} %get-tuple-element.11.values_ref, bf16[104,128,256]{2,1,0:T(8,128)(2,1)S(1)} %bitcast.10), custom_call_target="tpu_custom_call" | custom-call | tf_op jit(solution)/shard_map/block_products/pallas_call | solution.py:41
  43.5 0.0 copy-done
  43.5 90.7 %reduce_and_gather.1.panel = bf16[8,1664,256]{2,1,0:T(8,128)(2,1)S(1)} custom-call(f32[1]{0:T(128)S(6)} %copy.8.center, f32[1]{0:T(128)S(6)} %copy.9.width, bf16[4,4,1664,256]{3,2,1,0:T(8,128)(2,1)S(1)} %bitcast.9, bf16[1664,256]{1,0:T(8,128)(2,1)S(1)} %copy-done), custom_call_target="tpu_custom_call" | custom-call | tf_op jit(solution)/shard_map/reduce_and_gather/pallas_call | solution.py:514
  134.2 6.8 %block_products.3 = bf16[208,128,256]{2,1,0:T(8,128)(2,1)S(1)} custom-call(s32[1,256]{1,0:T(1,128)S(1)} %get-tuple-element.10.codes_ref, bf16[256,128,128]{2,1,0:T(8,128)(2,1)S(1)} %get-tuple-element.11.values_ref, bf16[104,128,256]{2,1,0:T(8,128)(2,1)S(1)} %bitcast.7), custom_call_target="tpu_custom_call" | custom-call | tf_op jit(solution)/shard_map/block_products/pallas_call | solution.py:41
  140.9 0.0 copy-start.1
  141.0 83.2 %reduce_and_swap.1 = (bf16[1664,256]{1,0:T(8,128)(2,1)S(1)}, bf16[832,256]{1,0:T(8,128)(2,1)S(1)}) custom-call(f32[1]{0:T(128)S(6)} %copy.8.center, f32[1]{0:T(128)S(6)} %copy.9.width, bf16[4,4,1664,256]{3,2,1,0:T(8,128)(2,1)S(1)} %bitcast.8, bf16[1664,256]{1,0:T(8,128)(2,1)S(1)} %copy-done, bf16[8,1664,256]{2,1,0:T(8,128)(2,1)S(1)} %reduce_and_gather.1.panel), custom_call_target="tpu_custom_call" | custom-call | tf_op jit(solution)/shard_map/reduce_and_swap/pallas_call | solution.py:527
  224.2 0.0 copy-done.1
  224.2 2.5 %place_rows.1 = bf16[2432,256]{1,0:T(8,128)(2,1)} custom-call(s32[128]{0:T(128)S(1)} %copy-done.1, bf16[1664,256]{1,0:T(8,128)(2,1)S(1)} %get-tuple-element.13.second, bf16[832,256]{1,0:T(8,128)(2,1)S(1)} %get-tuple-element.14.arriving), custom_call_target="tpu_custom_call" | custom-call | tf_op jit(solution)/shard_map/place_rows/pallas_call | solution.py:594
Async XLA Ops:
  36.7 6.8 %copy-start = (bf16[1664,256]{1,0:T(8,128)(2,1)S(1)}, bf16[1664,256]{1,0:T(8,128)(2,1)}, u32[]{:S(2)}) copy-start(bf16[1664,256]{1,0:T(8,128)(2,1)} %source.3) | copy-start | bytes 2555908
  140.9 83.2 %copy-start.1 = (s32[128]{0:T(128)S(1)}, s32[128]{0:T(128)}, u32[]{:S(2)}) copy-start(s32[128]{0:T(128)} %counts_ref.1) | copy-start | bytes 1540

commit v6 on v5

--- a/solution.py
+++ b/solution.py
@@ -11,13 +11,13 @@
 VECS = 256
 BD = 13
 MOVE = 6
-GROUP = 64
+GROUP = 128
 
 
 def product_kernel(codes_ref, values_ref, panel_ref, out_ref):
-    @pl.loop(0, out_ref.shape[0])
+    @pl.loop(0, out_ref.shape[0] // 8)
     def _(i):
-        out_ref[i] = jnp.zeros((ORB, VECS), jnp.bfloat16)
+        out_ref[pl.ds(8 * i, 8)] = jnp.zeros((8, ORB, VECS), jnp.bfloat16)
 
     def group(step, carry):
         before, total = carry

time: 227 us -> 226 us (level)
  no operation moved by 1% of the time
where the time goes in v6:
time: 226 us; the launch traced here: 225 us
  Pallas kernels  224 us (99%)
    pallas_call x1, Pallas kernels, first_of(): comm_call(first_kernel, 'reduce_and_gather', 1, LIMITS[1], [SCALAR, SCALA...  90.7 us
    pallas_call x1, Pallas kernels, second_of(): comm_call(second_kernel, 'reduce_and_swap', 2, LIMITS[2], [SCALAR, SCALAR...  83.2 us
    pallas_call x1, Pallas kernels, gathered(): comm_call(gather_kernel, 'gather_rows', 0, LIMITS[0], [HBM, HBM, HBM, HBM...  35.4 us
    pallas_call x2, Pallas kernels, cell_terms(): pl.pallas_call(product_kernel, out_shape=jax.ShapeDtypeStruct((out_blocks...  12.3 us

profile of v6, /device:TPU:8, one launch (start us, length us, event | category | flops | bytes accessed | tf_op | source)
XLA Modules:
  0.0 225.5 jit_solution(10531137909055262619)
XLA Ops:
  1.3 35.4 %gather_rows.1 = (bf16[8,1664,256]{2,1,0:T(8,128)(2,1)S(1)}, bf16[256,128,128]{2,1,0:T(8,128)(2,1)S(1)}, s32[1,256]{1,0:T(1,128)S(1)}) custom-call(s32[1,256]{1,0:T(1,128)} %bitcast.12, s32[1,256]{1,0:T(1,128)} %bitcast.13, bf16[1664,256]{1,0:T(8,128)(2,1)} %source.3, bf16[256,128,128]{2,1,0:T(8,128)(2,1)} %bitcast.11), custom_call_target="tpu_custom_call" | custom-call | tf_op jit(solution)/shard_map/gather_rows/pallas_call | solution.py:495
  36.7 0.0 copy-start
  36.7 6.2 %block_products.2 = bf16[208,128,256]{2,1,0:T(8,128)(2,1)S(1)} custom-call(s32[1,256]{1,0:T(1,128)S(1)} %get-tuple-element.10.codes_ref, bf16[256,128,128]{2,1,0:T(8,128)(2,1)S(1)} %get-tuple-element.11.values_ref, bf16[104,128,256]{2,1,0:T(8,128)(2,1)S(1)} %bitcast.10), custom_call_target="tpu_custom_call" | custom-call | tf_op jit(solution)/shard_map/block_products/pallas_call | solution.py:41
  42.9 0.0 copy-done
  42.9 90.7 %reduce_and_gather.1.panel = bf16[8,1664,256]{2,1,0:T(8,128)(2,1)S(1)} custom-call(f32[1]{0:T(128)S(6)} %copy.8.center, f32[1]{0:T(128)S(6)} %copy.9.width, bf16[4,4,1664,256]{3,2,1,0:T(8,128)(2,1)S(1)} %bitcast.9, bf16[1664,256]{1,0:T(8,128)(2,1)S(1)} %copy-done), custom_call_target="tpu_custom_call" | custom-call | tf_op jit(solution)/shard_map/reduce_and_gather/pallas_call | solution.py:514
  133.6 6.2 %block_products.3 = bf16[208,128,256]{2,1,0:T(8,128)(2,1)S(1)} custom-call(s32[1,256]{1,0:T(1,128)S(1)} %get-tuple-element.10.codes_ref, bf16[256,128,128]{2,1,0:T(8,128)(2,1)S(1)} %get-tuple-element.11.values_ref, bf16[104,128,256]{2,1,0:T(8,128)(2,1)S(1)} %bitcast.7), custom_call_target="tpu_custom_call" | custom-call | tf_op jit(solution)/shard_map/block_products/pallas_call | solution.py:41
  139.7 0.0 copy-start.1
  139.7 83.2 %reduce_and_swap.1 = (bf16[1664,256]{1,0:T(8,128)(2,1)S(1)}, bf16[832,256]{1,0:T(8,128)(2,1)S(1)}) custom-call(f32[1]{0:T(128)S(6)} %copy.8.center, f32[1]{0:T(128)S(6)} %copy.9.width, bf16[4,4,1664,256]{3,2,1,0:T(8,128)(2,1)S(1)} %bitcast.8, bf16[1664,256]{1,0:T(8,128)(2,1)S(1)} %copy-done, bf16[8,1664,256]{2,1,0:T(8,128)(2,1)S(1)} %reduce_and_gather.1.panel), custom_call_target="tpu_custom_call" | custom-call | tf_op jit(solution)/shard_map/reduce_and_swap/pallas_call | solution.py:527
  223.0 0.0 copy-done.1
  223.0 2.5 %place_rows.1 = bf16[2432,256]{1,0:T(8,128)(2,1)} custom-call(s32[128]{0:T(128)S(1)} %copy-done.1, bf16[1664,256]{1,0:T(8,128)(2,1)S(1)} %get-tuple-element.13.second, bf16[832,256]{1,0:T(8,128)(2,1)S(1)} %get-tuple-element.14.arriving), custom_call_target="tpu_custom_call" | custom-call | tf_op jit(solution)/shard_map/place_rows/pallas_call | solution.py:594
Async XLA Ops:
  36.7 6.2 %copy-start = (bf16[1664,256]{1,0:T(8,128)(2,1)S(1)}, bf16[1664,256]{1,0:T(8,128)(2,1)}, u32[]{:S(2)}) copy-start(bf16[1664,256]{1,0:T(8,128)(2,1)} %source.3) | copy-start | bytes 2555908
  139.7 83.2 %copy-start.1 = (s32[128]{0:T(128)S(1)}, s32[128]{0:T(128)}, u32[]{:S(2)}) copy-start(s32[128]{0:T(128)} %counts_ref.1) | copy-start | bytes 1540
